TPU v7x, 32 devices: a whole 2x2x4 slice. The times are simulated.
32 devices in a mesh: dp: 16 (over z, y, core), seq: 2 (over x).
Axes of the slice: x: 2, y: 2, z: 4, core: 2. Of those that a mesh axis runs over, the one named last changes fastest.
Arguments:
- clip_tokens: bfloat16 [16, 1024, 1024], P('dp', 'seq'), may hold values from -6 to 6
- adapter_index: int32 [16], P('dp'), may hold values from 0 to 7
- ln1_gain: float32 [1024], replicated, may hold values from 0.25 to 1.75
- ln1_bias: float32 [1024], replicated, may hold values from -1.8 to 1.8
- qkv_weight: bfloat16 [1024, 3072], replicated, may hold values from -0.1875 to 0.1875
- qkv_bias: float32 [3072], replicated, may hold values from -1.8 to 1.8
- qkv_down: bfloat16 [8, 16, 1024], replicated, may hold values from -0.1875 to 0.1875
- qkv_up: bfloat16 [8, 16, 3072], replicated, may hold values from -1.5 to 1.5
- out_weight: bfloat16 [1024, 1024], replicated, may hold values from -3 to 3
- out_bias: float32 [1024], replicated, may hold values from -1.8 to 1.8
- out_down: bfloat16 [8, 16, 1024], replicated, may hold values from -3 to 3
- out_up: bfloat16 [8, 16, 1024], replicated, may hold values from -1.5 to 1.5
- ln2_gain: float32 [1024], replicated, may hold values from 0.25 to 1.75
- ln2_bias: float32 [1024], replicated, may hold values from -1.8 to 1.8
- fc1_weight: bfloat16 [1024, 4096], replicated, may hold values from -0.1875 to 0.1875
- fc1_bias: float32 [4096], replicated, may hold values from -1.8 to 1.8
- fc1_down: bfloat16 [8, 16, 1024], replicated, may hold values from -0.1875 to 0.1875
- fc1_up: bfloat16 [8, 16, 4096], replicated, may hold values from -1.5 to 1.5
- fc2_weight: bfloat16 [4096, 1024], replicated, may hold values from -0.09375 to 0.09375
- fc2_bias: float32 [1024], replicated, may hold values from -1.8 to 1.8
- fc2_down: bfloat16 [8, 16, 4096], replicated, may hold values from -0.09375 to 0.09375
- fc2_up: bfloat16 [8, 16, 1024], replicated, may hold values from -1.5 to 1.5
- cotangent: bfloat16 [16, 1024, 1024], P('dp', 'seq'), may hold values from -6 to 6
Outputs:
- block_output: bfloat16 [16, 1024, 1024], P('dp', 'seq')
- input_grad: float32 [16, 1024, 1024], P('dp', 'seq')
- grad_qkv_down: float32 [8, 16, 1024], replicated
- grad_qkv_up: float32 [8, 16, 3072], replicated
- grad_out_down: float32 [8, 16, 1024], replicated
- grad_out_up: float32 [8, 16, 1024], replicated
- grad_fc1_down: float32 [8, 16, 1024], replicated
- grad_fc1_up: float32 [8, 16, 4096], replicated
- grad_fc2_down: float32 [8, 16, 4096], replicated
- grad_fc2_up: float32 [8, 16, 1024], replicated
All inputs are finite; a program needn't handle non-finite values.
Results may differ from a plain program's by a relative error of at most 0.023.
Values may be sent and summed in bfloat16 or wider, within the bound.
No kernel may reach another device: no remote copies, remote signals or barrier semaphores. Data moves between devices by JAX's collectives and lax.ppermute only.
A program may use at most 192 MiB of HBM per device.

v0:
```python
import jax
import jax.numpy as jnp
from jax import lax
from jax.sharding import PartitionSpec as P

HEADS = 16
HD = 64
FF = 4096
NADAPT = 8
GRID = 16


EPSILON = 1e-06
span_keys = 512


def norm_rows(values, gain, shift):
    centre = values - jnp.mean(values, axis=-1, keepdims=True)
    spread = lax.rsqrt(jnp.mean(centre * centre, axis=-1, keepdims=True) + EPSILON)
    normed = centre * spread
    return (normed * gain + shift, normed, spread)


def norm_back(grad_rows, normed, spread, gain):
    scaled = grad_rows * gain
    first_mean = jnp.mean(scaled, axis=-1, keepdims=True)
    second_mean = jnp.mean(scaled * normed, axis=-1, keepdims=True)
    return spread * (scaled - first_mean - normed * second_mean)


def rotary_tables(first_token, count_rows, head_size, grid_side):
    half_size = head_size // 2
    side_pairs = half_size // 3
    lead_pairs = half_size - 2 * side_pairs
    token_index = first_token + jnp.arange(count_rows, dtype=jnp.int32)
    frame = token_index // (grid_side * grid_side)
    row_pos = token_index // grid_side % grid_side
    col_pos = token_index % grid_side
    pair_index = jnp.arange(half_size, dtype=jnp.int32)
    axis_pick = jnp.where(
        pair_index < lead_pairs, 0, jnp.where(pair_index < lead_pairs + side_pairs, 1, 2)
    )
    local_pair = jnp.where(
        axis_pick == 0,
        pair_index,
        jnp.where(axis_pick == 1, pair_index - lead_pairs, pair_index - lead_pairs - side_pairs),
    )
    total_pairs = jnp.where(axis_pick == 0, lead_pairs, side_pairs)
    frequency = jnp.power(
        10000.0, -local_pair.astype(jnp.float32) / total_pairs.astype(jnp.float32)
    )
    position = jnp.where(
        axis_pick[None, :] == 0,
        frame[:, None],
        jnp.where(axis_pick[None, :] == 1, row_pos[:, None], col_pos[:, None]),
    ).astype(jnp.float32)
    angles = position * frequency[None, :]
    return (jnp.cos(angles), jnp.sin(angles))


def rotate(values, cosine, sine):
    half_size = values.shape[-1] // 2
    first_half = values[..., :half_size]
    second_half = values[..., half_size:]
    cos_rows = cosine[:, None, :]
    sin_rows = sine[:, None, :]
    return jnp.concatenate(
        [
            first_half * cos_rows - second_half * sin_rows,
            first_half * sin_rows + second_half * cos_rows,
        ],
        axis=-1,
    )


def unrotate(values, cosine, sine):
    half_size = values.shape[-1] // 2
    first_half = values[..., :half_size]
    second_half = values[..., half_size:]
    cos_rows = cosine[:, None, :]
    sin_rows = sine[:, None, :]
    return jnp.concatenate(
        [
            first_half * cos_rows + second_half * sin_rows,
            second_half * cos_rows - first_half * sin_rows,
        ],
        axis=-1,
    )


def project(inputs, weight, bias_row, down_pick, up_pick):
    low_rank = jnp.einsum(
        "crd,cad->cra", inputs, down_pick, preferred_element_type=jnp.float32
    ).astype(jnp.bfloat16)
    main_part = jnp.einsum("crd,de->cre", inputs, weight, preferred_element_type=jnp.float32)
    side_part = jnp.einsum("cra,cae->cre", low_rank, up_pick, preferred_element_type=jnp.float32)
    return (main_part + bias_row + side_part, low_rank)


def project_back(grad_low, inputs, low_rank, weight, down_pick, up_pick):
    main_part = jnp.einsum("cre,de->crd", grad_low, weight, preferred_element_type=jnp.float32)
    rank_grad = jnp.einsum(
        "cre,cae->cra", grad_low, up_pick, preferred_element_type=jnp.float32
    ).astype(jnp.bfloat16)
    backward = main_part + jnp.einsum(
        "cra,cad->crd", rank_grad, down_pick, preferred_element_type=jnp.float32
    )
    grad_up = jnp.einsum("cra,cre->cae", low_rank, grad_low, preferred_element_type=jnp.float32)
    grad_down = jnp.einsum("cra,crd->cad", rank_grad, inputs, preferred_element_type=jnp.float32)
    return (backward, grad_down, grad_up)


def over_blocks(block_step, carried, key_rows, value_rows, first_row):
    key_count = key_rows.shape[1]
    block_size = min(key_count, span_keys)
    full_blocks = key_count // block_size

    def one_block(number, inner):
        offset = number * block_size
        return block_step(
            inner,
            lax.dynamic_slice_in_dim(key_rows, offset, block_size, 1),
            lax.dynamic_slice_in_dim(value_rows, offset, block_size, 1),
            first_row + offset,
        )

    carried = lax.fori_loop(0, full_blocks, one_block, carried)
    return carried


def body(
    clip_tokens,
    adapter_index,
    ln1_gain,
    ln1_bias,
    qkv_weight,
    qkv_bias,
    qkv_down,
    qkv_up,
    out_weight,
    out_bias,
    out_down,
    out_up,
    ln2_gain,
    ln2_bias,
    fc1_weight,
    fc1_bias,
    fc1_down,
    fc1_up,
    fc2_weight,
    fc2_bias,
    fc2_down,
    fc2_up,
    cotangent,
):
    clip_count, row_count, model_width = clip_tokens.shape
    score_scale = HD ** (-0.5)
    head_shape = (clip_count, row_count, HEADS, HD)
    onehot = (adapter_index[:, None] == jnp.arange(NADAPT, dtype=jnp.int32)[None, :]).astype(
        jnp.bfloat16
    )

    def select(table_rows):
        return jnp.einsum(
            "ca,ard->crd", onehot, table_rows, preferred_element_type=jnp.float32
        ).astype(jnp.bfloat16)

    picks = [
        select(table_rows)
        for table_rows in (qkv_down, qkv_up, out_down, out_up, fc1_down, fc1_up, fc2_down, fc2_up)
    ]
    inputs = clip_tokens.astype(jnp.float32)
    first_norm, first_normed, first_spread = norm_rows(inputs, ln1_gain, ln1_bias)
    first_in = first_norm.astype(jnp.bfloat16)
    qkv_pre, rank_qkv = project(first_in, qkv_weight, qkv_bias, picks[0], picks[1])
    cosine, sine = rotary_tables(lax.axis_index("seq") * row_count, row_count, HD, GRID)
    query_heads = rotate(qkv_pre[..., :model_width].reshape(head_shape), cosine, sine).astype(
        jnp.bfloat16
    )
    key_low = (
        rotate(qkv_pre[..., model_width : 2 * model_width].reshape(head_shape), cosine, sine)
        .astype(jnp.bfloat16)
        .reshape(clip_count, row_count, model_width)
    )
    value_low = qkv_pre[..., 2 * model_width :].astype(jnp.bfloat16)

    def forward_step(carried, key_rows, value_rows, offset):
        row_max, row_sum, weighted = carried
        key_heads = key_rows.reshape(clip_count, key_rows.shape[1], HEADS, HD)
        value_heads = value_rows.reshape(clip_count, value_rows.shape[1], HEADS, HD)
        scores = (
            jnp.einsum(
                "cqhd,ckhd->chqk", query_heads, key_heads, preferred_element_type=jnp.float32
            )
            * score_scale
        )
        new_max = jnp.maximum(row_max, jnp.max(scores, axis=-1))
        weights = jnp.exp(scores - new_max[..., None])
        factor = jnp.exp(row_max - new_max)
        row_sum = row_sum * factor + jnp.sum(weights, axis=-1)
        update = jnp.einsum(
            "chqk,ckhd->cqhd",
            weights.astype(jnp.bfloat16),
            value_heads,
            preferred_element_type=jnp.float32,
        )
        weighted = weighted * jnp.transpose(factor, (0, 2, 1))[..., None] + update
        return (new_max, row_sum, weighted)

    init_state = (
        jnp.full((clip_count, HEADS, row_count), -1e30, jnp.float32),
        jnp.zeros((clip_count, HEADS, row_count), jnp.float32),
        jnp.zeros(head_shape, jnp.float32),
    )
    key_all, value_all = (
        lax.all_gather(key_low, "seq", axis=1, tiled=True),
        lax.all_gather(value_low, "seq", axis=1, tiled=True),
    )
    row_max, row_sum, weighted = over_blocks(forward_step, init_state, key_all, value_all, 0)
    out_heads = weighted / jnp.transpose(row_sum, (0, 2, 1))[..., None]
    log_total = row_max + jnp.log(row_sum)
    mixed_low = out_heads.reshape(clip_count, row_count, model_width).astype(jnp.bfloat16)
    attn_pre, rank_out = project(mixed_low, out_weight, out_bias, picks[2], picks[3])
    middle = inputs + attn_pre
    second_norm, second_normed, second_spread = norm_rows(middle, ln2_gain, ln2_bias)
    second_in = second_norm.astype(jnp.bfloat16)
    hidden, rank_fc1 = project(second_in, fc1_weight, fc1_bias, picks[4], picks[5])

    def exact_gelu(values):
        return jax.nn.gelu(values, approximate=False)

    active, gelu_back = jax.vjp(exact_gelu, hidden)
    active_low = active.astype(jnp.bfloat16)
    fc2_pre, rank_fc2 = project(active_low, fc2_weight, fc2_bias, picks[6], picks[7])
    block_output = (middle + fc2_pre).astype(jnp.bfloat16)
    grad_active, down_fc2, up_fc2 = project_back(
        cotangent, active_low, rank_fc2, fc2_weight, picks[6], picks[7]
    )
    grad_hidden = gelu_back(grad_active)[0].astype(jnp.bfloat16)
    grad_second, down_fc1, up_fc1 = project_back(
        grad_hidden, second_in, rank_fc1, fc1_weight, picks[4], picks[5]
    )
    grad_middle = cotangent.astype(jnp.float32) + norm_back(
        grad_second, second_normed, second_spread, ln2_gain
    )
    grad_mixed, down_out, up_out = project_back(
        grad_middle.astype(jnp.bfloat16), mixed_low, rank_out, out_weight, picks[2], picks[3]
    )
    grad_heads = grad_mixed.astype(jnp.bfloat16).reshape(head_shape)
    row_delta = jnp.transpose(
        jnp.sum(grad_heads.astype(jnp.float32) * out_heads, axis=-1), (0, 2, 1)
    )

    def score_block(query_rows, grad_rows, log_rows, delta_rows, key_heads, value_heads):
        scores = (
            jnp.einsum("cqhd,ckhd->chqk", query_rows, key_heads, preferred_element_type=jnp.float32)
            * score_scale
        )
        attn_prob = jnp.exp(scores - log_rows[..., None])
        grad_prob = jnp.einsum(
            "cqhd,ckhd->chqk", grad_rows, value_heads, preferred_element_type=jnp.float32
        )
        grad_score = (attn_prob * (grad_prob - delta_rows[..., None])).astype(jnp.bfloat16)
        return (attn_prob, grad_score)

    def backward_step(carried, key_rows, value_rows, offset):
        grad_query, key_full, value_full = carried
        key_heads = key_rows.reshape(clip_count, key_rows.shape[1], HEADS, HD)
        value_heads = value_rows.reshape(clip_count, value_rows.shape[1], HEADS, HD)
        attn_prob, grad_score = score_block(
            query_heads, grad_heads, log_total, row_delta, key_heads, value_heads
        )
        grad_query = (
            grad_query
            + jnp.einsum(
                "chqk,ckhd->cqhd", grad_score, key_heads, preferred_element_type=jnp.float32
            )
            * score_scale
        )
        key_part = (
            jnp.einsum(
                "chqk,cqhd->ckhd", grad_score, query_heads, preferred_element_type=jnp.float32
            )
            * score_scale
        )
        value_part = jnp.einsum(
            "chqk,cqhd->ckhd",
            attn_prob.astype(jnp.bfloat16),
            grad_heads,
            preferred_element_type=jnp.float32,
        )
        key_full = lax.dynamic_update_slice_in_dim(
            key_full, key_part.reshape(clip_count, key_rows.shape[1], model_width), offset, 1
        )
        value_full = lax.dynamic_update_slice_in_dim(
            value_full, value_part.reshape(clip_count, key_rows.shape[1], model_width), offset, 1
        )
        return (grad_query, key_full, value_full)

    whole_rows = row_count * lax.axis_size("seq")
    back_init = (
        jnp.zeros(head_shape, jnp.float32),
        jnp.zeros((clip_count, whole_rows, model_width), jnp.float32),
        jnp.zeros((clip_count, whole_rows, model_width), jnp.float32),
    )
    back_result = over_blocks(backward_step, back_init, key_all, value_all, 0)
    grad_query, key_full, value_full = back_result
    key_grad, value_grad = (
        lax.psum_scatter(
            key_full.astype(jnp.bfloat16), "seq", scatter_dimension=1, tiled=True
        ).astype(jnp.float32),
        lax.psum_scatter(
            value_full.astype(jnp.bfloat16), "seq", scatter_dimension=1, tiled=True
        ).astype(jnp.float32),
    )
    grad_qkv = jnp.concatenate(
        [
            unrotate(grad_query, cosine, sine).reshape(clip_count, row_count, model_width),
            unrotate(key_grad.reshape(head_shape), cosine, sine).reshape(
                clip_count, row_count, model_width
            ),
            value_grad,
        ],
        axis=-1,
    ).astype(jnp.bfloat16)
    grad_first, down_qkv, up_qkv = project_back(
        grad_qkv, first_in, rank_qkv, qkv_weight, picks[0], picks[1]
    )
    input_grad = grad_middle + norm_back(grad_first, first_normed, first_spread, ln1_gain)
    packed_clip = jnp.concatenate(
        [down_qkv, up_qkv, down_out, up_out, down_fc1, up_fc1, down_fc2, up_fc2], axis=2
    )
    packed = jnp.einsum(
        "ca,crw->arw", onehot.astype(jnp.float32), packed_clip, precision=lax.Precision.HIGHEST
    )
    summed = lax.psum(packed.astype(jnp.bfloat16), "dp")
    owned = lax.psum_scatter(summed, "seq", scatter_dimension=2, tiled=True).astype(jnp.float32)
    gathered = lax.all_gather(owned.astype(jnp.bfloat16), "seq", axis=2, tiled=True).astype(
        owned.dtype
    )
    widths = [
        model_width,
        3 * model_width,
        model_width,
        model_width,
        model_width,
        FF,
        FF,
        model_width,
    ]
    results = []
    position = 0
    for span_width in widths:
        results.append(gathered[:, :, position : position + span_width])
        position = position + span_width
    return (
        block_output,
        input_grad,
        results[0],
        results[1],
        results[2],
        results[3],
        results[4],
        results[5],
        results[6],
        results[7],
    )


def solution(mesh):
    return jax.shard_map(
        body,
        mesh=mesh,
        in_specs=(
            P("dp", "seq", None),
            P("dp"),
            P(),
            P(),
            P(),
            P(),
            P(),
            P(),
            P(),
            P(),
            P(),
            P(),
            P(),
            P(),
            P(),
            P(),
            P(),
            P(),
            P(),
            P(),
            P(),
            P(),
            P("dp", "seq", None),
        ),
        out_specs=(
            P("dp", "seq", None),
            P("dp", "seq", None),
            P(),
            P(),
            P(),
            P(),
            P(),
            P(),
            P(),
            P(),
        ),
        check_vma=False,
    )
```

profile of v0, /device:TPU:0, one launch (start us, length us, event | category | flops | bytes accessed | tf_op | source)
XLA Modules:
  0.0 613.7 jit_solution(2214221213722635700)
XLA Ops:
  7.2 1.6 convert_reduce_fusion
  8.8 1.6 fusion.44
  12.4 6.8 %fusion.113 = f32[512,3072]{1,0:T(8,128)S(1)} fusion(bf16[1024,3072]{1,0:T(8,128)(2,1)} %param.31, bf16[1,512,1024]{2,1,0:T(8,128)(2,1)} %param.27, f32[1024]{0:T(1024)} %param.30, f32[1024]{0:T(1024)} %param.29, f32[512]{0:T(512)S(1)} %add_rsqrt_fusion.1, f32[512]{0:T(512)S(1)} %broadcast_multiply_fusion.5), kind=kOutput, calls=%fused_computation.224 | convolution fusion | flops 3224371200 | bytes 13643776 | tf_op jit(solution)/shard_map/crd,de->cre/dot_general | solution.py:95
  21.6 2.6 copy-done.13
  25.5 4.8 fusion.116
  30.3 2.9 copy.44
  33.2 3.0 copy.43
  36.6 4.2 subtract_convert_fusion.2
  42.9 1.8 fusion.75
  46.9 1.8 fusion.73
  50.1 2.5 fusion.66
  52.7 3.2 fusion.64
  55.9 10.4 %fusion.62 = f32[512,4096]{1,0:T(8,128)} fusion(bf16[4096,1024]{1,0:T(8,128)(2,1)} %param.45, bf16[1,512,1024]{2,1,0:T(8,128)(2,1)S(1)} %copy-done.23), kind=kOutput, calls=%fused_computation.125 | convolution fusion | flops 4294967296 | bytes 17825792 | tf_op jit(solution)/shard_map/cre,de->crd/dot_general | solution.py:101
  66.3 3.9 copy.45
  70.2 26.5 %all-gather.4.cloned.1.call-done = bf16[1,1024,1024]{1,2,0:T(8,128)(2,1)} async-done(((bf16[1,512,1024]{1,2,0:T(8,128)(2,1)}), bf16[1,1024,1024]{1,2,0:T(8,128)(2,1)}) %all-gather.4.cloned.1.call-update) | async-done | bytes 2097168 | tf_op jit(solution)/shard_map/all_gather | solution.py:216
  96.6 60.7 %while.36 = (s32[]{:T(128)}, f32[1,16,512]{2,1,0:T(8,128)S(1)}, f32[1,16,512]{2,1,0:T(8,128)S(1)}, f32[1,512,16,64]{1,3,2,0:T(8,128)}, bf16[1,1024,1024]{1,2,0:T...) while((s32[]{:T(128)}, f32[1,16,512]{2,1,0:T(8,128)S(1)}, ...), condition=%wide.region_5.6_spmd.clone, body=%wide.region_2.5_spmd.clone.sunk | while | flops 1108918272 | bytes 66584780 | solution.py:127
  96.6 2.6 constant_dynamic-slice_fusion.7
  99.3 8.2 %bitcast_reduce_fusion.2 = (f32[16,512]{1,0:T(8,128)S(1)}, f32[16,512,512]{2,1,0:T(8,128)}) fusion(bf16[512,16,64]{0,2,1:T(8,128)(2,1)S(1)} %bitcast.339, bf16[1,512,16,64]{1,3,2,0:T(8,128)(2,1)S(1)} %get-tuple-element.629), kind=kOutput, calls=%fused_computation.1.clone.1 | convolution fusion | flops 545251328 | bytes 18907136 | tf_op jit(solution)/shard_map/while/body/eval_jaxpr/cqhd,ckhd->chqk/dot_general | solution.py:192
  107.5 8.7 %fusion.188 = f32[16,512]{1,0:T(8,128)S(1)} fusion(f32[16,512,512]{2,1,0:T(8,128)} %get-tuple-element.587, f32[16,512]{1,0:T(8,128)S(1)} %bitcast.342), kind=kLoop, calls=%fused_computation.4.clone.1 | loop fusion | flops 12574720 | bytes 16842752 | tf_op jit(solution)/shard_map/while/body/eval_jaxpr/reduce_sum | solution.py:200
  116.2 10.3 %bitcast_add_fusion.8 = f32[1,512,16,64]{1,3,2,0:T(8,128)} fusion(f32[1,512,16,64]{1,3,2,0:T(8,128)} %get-tuple-element.616, bf16[512,16,64]{0,2,1:T(8,128)(2,1)S(1)} %bitcast.337, f32[16,512,512]{2,1,0:T(8,128)} %get-tuple-element.587, f32[16,512]{1,0:T(8,128)S(1)} %bitcast.343, f32[512,16]{0,1:T(8,128)S(1)} %get-tuple-element.589, pred[]{:T(512)S(6)} %compare.27), kind=kOutput, calls=%fused_computation.8.clone.1 | convolution fusion | flops 551026688 | bytes 22085632 | tf_op jit(solution)/shard_map/while/body/eval_jaxpr/chqk,ckhd->cqhd/dot_general | solution.py:201
  126.5 2.6 constant_dynamic-slice_fusion.7
  129.1 8.2 %bitcast_reduce_fusion.2 = (f32[16,512]{1,0:T(8,128)S(1)}, f32[16,512,512]{2,1,0:T(8,128)}) fusion(bf16[512,16,64]{0,2,1:T(8,128)(2,1)S(1)} %bitcast.339, bf16[1,512,16,64]{1,3,2,0:T(8,128)(2,1)S(1)} %get-tuple-element.629), kind=kOutput, calls=%fused_computation.1.clone.1 | convolution fusion | flops 545251328 | bytes 18907136 | tf_op jit(solution)/shard_map/while/body/eval_jaxpr/cqhd,ckhd->chqk/dot_general | solution.py:192
  137.4 8.7 %fusion.188 = f32[16,512]{1,0:T(8,128)S(1)} fusion(f32[16,512,512]{2,1,0:T(8,128)} %get-tuple-element.587, f32[16,512]{1,0:T(8,128)S(1)} %bitcast.342), kind=kLoop, calls=%fused_computation.4.clone.1 | loop fusion | flops 12574720 | bytes 16842752 | tf_op jit(solution)/shard_map/while/body/eval_jaxpr/reduce_sum | solution.py:200
  146.1 10.9 %bitcast_add_fusion.8 = f32[1,512,16,64]{1,3,2,0:T(8,128)} fusion(f32[1,512,16,64]{1,3,2,0:T(8,128)} %get-tuple-element.616, bf16[512,16,64]{0,2,1:T(8,128)(2,1)S(1)} %bitcast.337, f32[16,512,512]{2,1,0:T(8,128)} %get-tuple-element.587, f32[16,512]{1,0:T(8,128)S(1)} %bitcast.343, f32[512,16]{0,1:T(8,128)S(1)} %get-tuple-element.589, pred[]{:T(512)S(6)} %compare.27), kind=kOutput, calls=%fused_computation.8.clone.1 | convolution fusion | flops 551026688 | bytes 22085632 | tf_op jit(solution)/shard_map/while/body/eval_jaxpr/chqk,ckhd->cqhd/dot_general | solution.py:201
  157.4 2.0 fusion.68
  163.8 1.7 slice-done.1
  165.5 4.5 fusion.121
  170.0 21.3 %multiply_convert_fusion.2 = (bf16[512,4096]{1,0:T(8,128)(2,1)}, f32[512,4096]{1,0:T(8,128)}, f32[512,4096]{1,0:T(8,128)}) fusion(bf16[512,16]{0,1:T(8,128)(2,1)S(1)} %convolution_convert_fusion.4, bf16[1,16,4096]{2,0,1:T(2,128)(2,1)S(1)} %fusion.66, f32[512,4096]{1,0:T(8,128)S(1)} %fusion.121, f32[4096]{0:T(1024)S(1)} %copy-done.76), kind=kOutput, calls=%fused_computation.42 | convolution fusion | flops 207618048 | bytes 29523968 | tf_op jit(solution)/shard_map/cra,cae->cre/dot_general | solution.py:96
  191.4 10.5 %add_convert_fusion = bf16[512,4096]{1,0:T(8,128)(2,1)S(1)} fusion(f32[512,4096]{1,0:T(8,128)} %get-tuple-element.441, f32[512,4096]{1,0:T(8,128)} %fusion.62, f32[512,4096]{1,0:T(8,128)} %get-tuple-element.473, bf16[16,512]{1,0:T(8,128)(2,1)S(1)} %copy-done.57, bf16[1,16,4096]{2,0,1:T(2,128)(2,1)S(1)} %copy-done.38), kind=kOutput, calls=%fused_computation.41 | convolution fusion | flops 98566144 | bytes 29507584 | tf_op jit(solution)/shard_map/cra,cad->crd/dot_general | solution.py:105
  201.9 4.5 fusion.123
  207.6 2.0 fusion.45
  209.6 1.8 reduce_sum.100
  211.4 3.2 fusion.47
  218.0 2.0 multiply_reduce_fusion
  220.0 1.6 broadcast.568
  221.6 1.6 broadcast.568.clone
  223.2 85.0 %while.37 = (s32[]{:T(128)}, f32[1,512,16,64]{1,3,2,0:T(8,128)}, bf16[1,1024,1024]{1,2,0:T(8,128)(2,1)}, bf16[1,1024,1024]{1,2,0:T(8,128)(2,1)}, bf16[1,1024,102...) while((s32[]{:T(128)}, f32[1,512,16,64]{1,3,2,0:T(8,128)}, ...), condition=%wide.region_12.13_spmd.clone, body=%wide.region_11.12_spmd.clone.sunk | while | flops 2720530432 | bytes 139559264 | solution.py:127
  224.7 8.2 %fusion.199 = f32[16,512,512]{2,1,0:T(8,128)} fusion(bf16[512,16,64]{0,2,1:T(8,128)(2,1)S(1)} %bitcast.333, bf16[1,512,16,64]{1,3,2,0:T(8,128)(2,1)S(1)} %get-tuple-element.668), kind=kOutput, calls=%fused_computation.33.clone.1 | convolution fusion | flops 536870912 | bytes 18874368 | tf_op jit(solution)/shard_map/while/body/eval_jaxpr/cqhd,ckhd->chqk/dot_general | solution.py:256
  233.0 10.2 %multiply_convert_fusion.4 = bf16[16,512,512]{2,1,0:T(8,128)(2,1)} fusion(f32[16,512,512]{2,1,0:T(8,128)} %fusion.199, bf16[512,16,64]{0,2,1:T(8,128)(2,1)S(1)} %bitcast.340, f32[16,512]{1,0:T(8,128)S(1)} %bitcast.355, f32[16,512]{1,0:T(8,128)S(1)} %bitcast.350, bf16[1,512,16,64]{1,3,2,0:T(8,128)(2,1)S(1)} %get-tuple-element.671), kind=kOutput, calls=%fused_computation.20.clone.1 | convolution fusion | flops 557842432 | bytes 27328512 | tf_op jit(solution)/shard_map/while/body/eval_jaxpr/cqhd,ckhd->chqk/dot_general | solution.py:260
  243.3 6.2 %bitcast_add_fusion.9 = f32[1,512,16,64]{1,3,2,0:T(8,128)} fusion(f32[1,512,16,64]{1,3,2,0:T(8,128)} %get-tuple-element.650, bf16[512,16,64]{0,2,1:T(8,128)(2,1)S(1)} %bitcast.334, bf16[16,512,512]{2,1,0:T(8,128)(2,1)} %multiply_convert_fusion.4, pred[]{:T(512)S(6)} %compare.28), kind=kOutput, calls=%fused_computation.28.clone.1 | convolution fusion | flops 538443776 | bytes 13631489 | tf_op jit(solution)/shard_map/while/body/eval_jaxpr/chqk,ckhd->cqhd/dot_general | solution.py:275
  249.4 7.5 %fusion.200 = bf16[16,512,64]{1,2,0:T(8,128)(2,1)S(1)} fusion(f32[16,512,512]{2,1,0:T(8,128)} %fusion.199, f32[16,512]{1,0:T(8,128)S(1)} %bitcast.351, bf16[1,512,16,64]{1,3,2,0:T(8,128)(2,1)S(1)} %get-tuple-element.671), kind=kOutput, calls=%fused_computation.23.clone.1 | convolution fusion | flops 549453824 | bytes 18907136 | tf_op jit(solution)/shard_map/while/body/eval_jaxpr/chqk,cqhd->ckhd/dot_general | solution.py:286
  257.0 6.2 %convolution_multiply_fusion.2 = bf16[16,512,64]{1,2,0:T(8,128)(2,1)S(1)} fusion(bf16[16,512,512]{2,1,0:T(8,128)(2,1)} %multiply_convert_fusion.4, bf16[1,512,16,64]{1,3,2,0:T(8,128)(2,1)S(1)} %get-tuple-element.668), kind=kOutput, calls=%fused_computation.29.clone.1 | convolution fusion | flops 537919488 | bytes 10485760 | tf_op jit(solution)/shard_map/while/body/eval_jaxpr/chqk,cqhd->ckhd/dot_general | solution.py:281
  266.8 8.2 %fusion.199 = f32[16,512,512]{2,1,0:T(8,128)} fusion(bf16[512,16,64]{0,2,1:T(8,128)(2,1)S(1)} %bitcast.333, bf16[1,512,16,64]{1,3,2,0:T(8,128)(2,1)S(1)} %get-tuple-element.668), kind=kOutput, calls=%fused_computation.33.clone.1 | convolution fusion | flops 536870912 | bytes 18874368 | tf_op jit(solution)/shard_map/while/body/eval_jaxpr/cqhd,ckhd->chqk/dot_general | solution.py:256
  275.1 10.2 %multiply_convert_fusion.4 = bf16[16,512,512]{2,1,0:T(8,128)(2,1)} fusion(f32[16,512,512]{2,1,0:T(8,128)} %fusion.199, bf16[512,16,64]{0,2,1:T(8,128)(2,1)S(1)} %bitcast.340, f32[16,512]{1,0:T(8,128)S(1)} %bitcast.355, f32[16,512]{1,0:T(8,128)S(1)} %bitcast.350, bf16[1,512,16,64]{1,3,2,0:T(8,128)(2,1)S(1)} %get-tuple-element.671), kind=kOutput, calls=%fused_computation.20.clone.1 | convolution fusion | flops 557842432 | bytes 27328512 | tf_op jit(solution)/shard_map/while/body/eval_jaxpr/cqhd,ckhd->chqk/dot_general | solution.py:260
  285.4 6.8 %bitcast_add_fusion.9 = f32[1,512,16,64]{1,3,2,0:T(8,128)} fusion(f32[1,512,16,64]{1,3,2,0:T(8,128)} %get-tuple-element.650, bf16[512,16,64]{0,2,1:T(8,128)(2,1)S(1)} %bitcast.334, bf16[16,512,512]{2,1,0:T(8,128)(2,1)} %multiply_convert_fusion.4, pred[]{:T(512)S(6)} %compare.28), kind=kOutput, calls=%fused_computation.28.clone.1 | convolution fusion | flops 538443776 | bytes 13631489 | tf_op jit(solution)/shard_map/while/body/eval_jaxpr/chqk,ckhd->cqhd/dot_general | solution.py:275
  292.1 7.5 %fusion.200 = bf16[16,512,64]{1,2,0:T(8,128)(2,1)S(1)} fusion(f32[16,512,512]{2,1,0:T(8,128)} %fusion.199, f32[16,512]{1,0:T(8,128)S(1)} %bitcast.351, bf16[1,512,16,64]{1,3,2,0:T(8,128)(2,1)S(1)} %get-tuple-element.671), kind=kOutput, calls=%fused_computation.23.clone.1 | convolution fusion | flops 549453824 | bytes 18907136 | tf_op jit(solution)/shard_map/while/body/eval_jaxpr/chqk,cqhd->ckhd/dot_general | solution.py:286
  299.7 6.2 %convolution_multiply_fusion.2 = bf16[16,512,64]{1,2,0:T(8,128)(2,1)S(1)} fusion(bf16[16,512,512]{2,1,0:T(8,128)(2,1)} %multiply_convert_fusion.4, bf16[1,512,16,64]{1,3,2,0:T(8,128)(2,1)S(1)} %get-tuple-element.668), kind=kOutput, calls=%fused_computation.29.clone.1 | convolution fusion | flops 537919488 | bytes 10485760 | tf_op jit(solution)/shard_map/while/body/eval_jaxpr/chqk,cqhd->ckhd/dot_general | solution.py:281
  309.2 3.5 convolution_convert_fusion.7
  312.7 27.5 %reduce-scatter.4.cloned.1.call-done = bf16[1,512,1024]{1,2,0:T(8,128)(2,1)} async-done(((bf16[1,1024,1024]{1,2,0:T(8,128)(2,1)}), bf16[1,512,1024]{1,2,0:T(8,128)(2,1)}) %reduce-scatter.4.cloned.1.call-update) | async-done | bytes 1048592 | tf_op jit(solution)/shard_map/reduce_scatter | solution.py:309
  340.2 1.5 convert.54
  342.7 31.6 %reduce-scatter.6.cloned.1.call-done = bf16[1,512,1024]{1,2,0:T(8,128)(2,1)} async-done(((bf16[1,1024,1024]{1,2,0:T(8,128)(2,1)}), bf16[1,512,1024]{1,2,0:T(8,128)(2,1)}) %reduce-scatter.6.cloned.1.call-update) | async-done | bytes 1048592 | tf_op jit(solution)/shard_map/reduce_scatter | solution.py:312
  374.3 1.8 convolution_convert_fusion
  376.8 2.6 fusion.32
  383.2 2.6 multiply_convert_fusion.1
  385.9 54.4 %reduce-scatter.8.cloned.1.call-done = bf16[8,16,8192]{2,1,0:T(8,128)(2,1)} async-done(((bf16[8,16,16384]{2,1,0:T(8,128)(2,1)}), bf16[8,16,8192]{2,1,0:T(8,128)(2,1)}) %reduce-scatter.8.cloned.1.call-update) | async-done | bytes 2097168 | tf_op jit(solution)/shard_map/reduce_scatter | solution.py:337
  440.7 101.3 %all-reduce.2.cloned.1.call-done = bf16[8,16,8192]{2,1,0:T(8,128)(2,1)} async-done(((bf16[8,16,8192]{2,1,0:T(8,128)(2,1)}), bf16[8,16,8192]{2,1,0:T(8,128)(2,1)}) %all-reduce.2.cloned.1.call-update) | async-done | bytes 2097168 | tf_op jit(solution)/shard_map/psum | solution.py:336
  542.1 8.3 %fusion.122 = f32[512,1024]{1,0:T(8,128)S(1)} fusion(bf16[512,4096]{1,0:T(8,128)(2,1)} %get-tuple-element.440, bf16[4096,1024]{1,0:T(8,128)(2,1)} %param.45), kind=kOutput, calls=%fused_computation.231 | convolution fusion | flops 4294967296 | bytes 14680064 | tf_op jit(solution)/shard_map/crd,de->cre/dot_general | solution.py:95
  553.0 6.8 %fusion.110 = f32[512,1024]{1,0:T(8,128)S(1)} fusion(bf16[1024,3072]{1,0:T(8,128)(2,1)} %param.31, bf16[512,1024]{0,1:T(8,128)(2,1)S(1)} %bitcast.368, bf16[512,1024]{0,1:T(8,128)(2,1)S(1)} %bitcast.359, bf16[512,1024]{0,1:T(8,128)(2,1)S(1)} %bitcast.362), kind=kOutput, calls=%fused_computation.223 | convolution fusion | flops 3230662656 | bytes 11534336 | tf_op jit(solution)/shard_map/cre,de->crd/dot_general | solution.py:101
  559.8 2.0 fusion.40
  561.8 1.8 reduce_sum.104
  563.6 3.5 fusion.43
  567.2 32.4 %all-gather.8.cloned.1.call-done = bf16[8,16,16384]{2,1,0:T(8,128)(2,1)} async-done(((bf16[8,16,8192]{2,1,0:T(8,128)(2,1)}), bf16[8,16,16384]{2,1,0:T(8,128)(2,1)}) %all-gather.8.cloned.1.call-update) | async-done | bytes 4194320 | tf_op jit(solution)/shard_map/all_gather | solution.py:338
  599.6 3.0 fusion.117
  603.9 2.5 fusion.118
  (252 shorter events, 37.7 us)
Async XLA Ops:
  7.2 153.3 %copy-start = (bf16[1024,1024]{1,0:T(8,128)(2,1)S(1)}, bf16[1024,1024]{1,0:T(8,128)(2,1)}, u32[]{:S(2)}) copy-start(bf16[1024,1024]{1,0:T(8,128)(2,1)} %param.35) | copy-start | bytes 6291460
  7.2 59.1 %all-gather.6.cloned.1.call-start = ((), (), s32[]{:S(2)}) async-start(), calls=%async_computation.4 | async-start | bytes 3145728 | tf_op jit(solution)/shard_map/all_gather | solution.py:217
  8.8 10.5 %copy-start.61 = (f32[512]{0:T(512)}, f32[512]{0:T(512)S(1)}, u32[]{:S(2)}) copy-start(f32[512]{0:T(512)S(1)} %broadcast_multiply_fusion.5) | copy-start | bytes 6148
  10.5 8.8 %copy-start.63 = (f32[512]{0:T(512)}, f32[512]{0:T(512)S(1)}, u32[]{:S(2)}) copy-start(f32[512]{0:T(512)S(1)} %add_rsqrt_fusion.1) | copy-start | bytes 6148
  12.4 6.9 %copy-start.55 = (bf16[1,16,1024]{2,0,1:T(2,128)(2,1)}, bf16[1,16,1024]{2,0,1:T(2,128)(2,1)S(1)}, u32[]{:S(2)}) copy-start(bf16[1,16,1024]{2,0,1:T(2,128)(2,1)S(1)} %fusion.79) | copy-start | bytes 98308
  12.4 6.9 %copy-start.10 = (bf16[1,512,1024]{2,1,0:T(8,128)(2,1)S(1)}, bf16[1,512,1024]{2,1,0:T(8,128)(2,1)}, u32[]{:S(2)}) copy-start(bf16[1,512,1024]{2,1,0:T(8,128)(2,1)} %param.27) | copy-start | bytes 3145732
  12.4 6.9 %copy-start.70 = (f32[1024]{0:T(1024)S(1)}, f32[1024]{0:T(1024)}, u32[]{:S(2)}) copy-start(f32[1024]{0:T(1024)} %param.29) | copy-start | bytes 12292
  12.4 6.9 %copy-start.77 = (f32[1024]{0:T(1024)S(1)}, f32[1024]{0:T(1024)}, u32[]{:S(2)}) copy-start(f32[1024]{0:T(1024)} %param.30) | copy-start | bytes 12292
  12.4 7.5 %copy-start.33 = (bf16[8,16,3072]{2,1,0:T(8,128)(2,1)S(1)}, bf16[8,16,3072]{2,1,0:T(8,128)(2,1)}, u32[]{:S(2)}) copy-start(bf16[8,16,3072]{2,1,0:T(8,128)(2,1)} %param.34) | copy-start | bytes 2359300
  12.4 8.2 %copy-start.68 = (f32[3072]{0:T(1024)S(1)}, f32[3072]{0:T(1024)}, u32[]{:S(2)}) copy-start(f32[3072]{0:T(1024)} %param.32) | copy-start | bytes 36868
  25.4 71.2 %all-gather.4.cloned.1.call-start = ((), (), s32[]{:S(2)}) async-start(), calls=%async_computation.3 | async-start | bytes 3145728 | tf_op jit(solution)/shard_map/all_gather | solution.py:216
  36.6 5.3 copy-start.34
  36.6 5.3 copy-start.36
  36.6 5.3 copy-start.48
  36.6 9.3 %copy-start.22 = (bf16[1,512,1024]{2,1,0:T(8,128)(2,1)S(1)}, bf16[1,512,1024]{2,1,0:T(8,128)(2,1)}, u32[]{:S(2)}) copy-start(bf16[1,512,1024]{2,1,0:T(8,128)(2,1)} %param.49) | copy-start | bytes 3145732
  41.9 298.3 %reduce-scatter.4.cloned.1.call-start = ((), (), s32[]{:S(2)}) async-start(), calls=%async_computation.5 | async-start | bytes 3145728 | tf_op jit(solution)/shard_map/reduce_scatter | solution.py:309
  48.7 7.1 %copy-start.23 = (bf16[1,512,1024]{2,1,0:T(8,128)(2,1)S(1)}, bf16[1,512,1024]{2,1,0:T(8,128)(2,1)}, u32[]{:S(2)}) copy-start(bf16[1,512,1024]{2,1,0:T(8,128)(2,1)} %param.49) | copy-start | bytes 3145732
  107.5 8.7 %copy-start.3 = (bf16[1,512,1024]{1,2,0:T(8,128)(2,1)S(1)}, bf16[1,512,1024]{1,2,0:T(8,128)(2,1)}, u32[]{:S(2)}) copy-start(bf16[1,512,1024]{1,2,0:T(8,128)(2,1)} %get-tuple-element.588) | copy-start | bytes 3145732 | tf_op jit(solution)/shard_map/while
  137.3 8.7 %copy-start.3 = (bf16[1,512,1024]{1,2,0:T(8,128)(2,1)S(1)}, bf16[1,512,1024]{1,2,0:T(8,128)(2,1)}, u32[]{:S(2)}) copy-start(bf16[1,512,1024]{1,2,0:T(8,128)(2,1)} %get-tuple-element.588) | copy-start | bytes 3145732 | tf_op jit(solution)/shard_map/while
  157.3 4.5 copy-start.11
  157.3 4.5 copy-start.42
  157.4 4.5 copy-start.72
  160.5 3.3 slice-start
  161.9 3.6 slice-start.1
  162.6 45.0 %copy-start.5 = (f32[1,512,1024]{2,1,0:T(8,128)}, f32[1,512,1024]{2,1,0:T(8,128)S(1)}, u32[]{:S(2)}) copy-start(f32[1,512,1024]{2,1,0:T(8,128)S(1)} %get-tuple-element.472) | copy-start | bytes 6291460
  163.4 6.6 %copy-start.20 = (bf16[512,1024]{1,0:T(8,128)(2,1)}, bf16[512,1024]{1,0:T(8,128)(2,1)S(1)}, u32[]{:S(2)}) copy-start(bf16[512,1024]{1,0:T(8,128)(2,1)S(1)} %fusion.54) | copy-start | bytes 3145732
  165.5 4.5 copy-start.59
  165.5 4.5 copy-start.76
  170.0 21.3 %copy-start.38 = (bf16[1,16,4096]{2,0,1:T(2,128)(2,1)S(1)}, bf16[1,16,4096]{2,0,1:T(2,128)(2,1)}, u32[]{:S(2)}) copy-start(bf16[1,16,4096]{2,0,1:T(2,128)(2,1)} %fusion.64) | copy-start | bytes 393220
  170.0 21.3 %copy-start.57 = (bf16[16,512]{1,0:T(8,128)(2,1)S(1)}, bf16[16,512]{1,0:T(8,128)(2,1)}, u32[]{:S(2)}) copy-start(bf16[16,512]{1,0:T(8,128)(2,1)} %convolution_convert_fusion.3) | copy-start | bytes 49156
  201.9 4.5 copy-start.17
  207.6 3.8 copy-start.51
  224.7 8.2 %copy-start.4 = (bf16[1,1024,1024]{1,2,0:T(8,128)(2,1)S(1)}, bf16[1,1024,1024]{1,2,0:T(8,128)(2,1)}, u32[]{:S(2)}) copy-start(bf16[1,1024,1024]{1,2,0:T(8,128)(2,1)} %get-tuple-element.670) | copy-start | bytes 6291460 | tf_op jit(solution)/shard_map/while
  256.9 6.2 %copy-start.25 = (bf16[1,1024,1024]{1,2,0:T(8,128)(2,1)S(1)}, bf16[1,1024,1024]{1,2,0:T(8,128)(2,1)}, u32[]{:S(2)}) copy-start(bf16[1,1024,1024]{1,2,0:T(8,128)(2,1)} %get-tuple-element.651) | copy-start | bytes 6291460 | tf_op jit(solution)/shard_map/while
  257.0 6.2 %copy-start.27 = (bf16[1,1024,1024]{1,2,0:T(8,128)(2,1)S(1)}, bf16[1,1024,1024]{1,2,0:T(8,128)(2,1)}, u32[]{:S(2)}) copy-start(bf16[1,1024,1024]{1,2,0:T(8,128)(2,1)} %get-tuple-element.652) | copy-start | bytes 6291460 | tf_op jit(solution)/shard_map/while
  266.8 8.2 %copy-start.4 = (bf16[1,1024,1024]{1,2,0:T(8,128)(2,1)S(1)}, bf16[1,1024,1024]{1,2,0:T(8,128)(2,1)}, u32[]{:S(2)}) copy-start(bf16[1,1024,1024]{1,2,0:T(8,128)(2,1)} %get-tuple-element.670) | copy-start | bytes 6291460 | tf_op jit(solution)/shard_map/while
  299.6 6.2 %copy-start.25 = (bf16[1,1024,1024]{1,2,0:T(8,128)(2,1)S(1)}, bf16[1,1024,1024]{1,2,0:T(8,128)(2,1)}, u32[]{:S(2)}) copy-start(bf16[1,1024,1024]{1,2,0:T(8,128)(2,1)} %get-tuple-element.651) | copy-start | bytes 6291460 | tf_op jit(solution)/shard_map/while
  299.6 6.2 %copy-start.27 = (bf16[1,1024,1024]{1,2,0:T(8,128)(2,1)S(1)}, bf16[1,1024,1024]{1,2,0:T(8,128)(2,1)}, u32[]{:S(2)}) copy-start(bf16[1,1024,1024]{1,2,0:T(8,128)(2,1)} %get-tuple-element.652) | copy-start | bytes 6291460 | tf_op jit(solution)/shard_map/while
  308.2 66.0 %reduce-scatter.6.cloned.1.call-start = ((), (), s32[]{:S(2)}) async-start(), calls=%async_computation.6 | async-start | bytes 3145728 | tf_op jit(solution)/shard_map/reduce_scatter | solution.py:312
  308.8 32.9 %copy-start.2 = (f32[1,512,16,64]{1,3,2,0:T(8,128)S(1)}, f32[1,512,16,64]{1,3,2,0:T(8,128)}, u32[]{:S(2)}) copy-start(f32[1,512,16,64]{1,3,2,0:T(8,128)} %get-tuple-element.310) | copy-start | bytes 6291460
  308.8 32.9 %copy-start.35 = (f32[512,32]{0,1:T(8,128)S(1)}, f32[512,32]{0,1:T(8,128)}, u32[]{:S(2)}) copy-start(f32[512,32]{0,1:T(8,128)} %copy-done.34) | copy-start | bytes 196612
  308.8 32.9 %copy-start.37 = (f32[512,32]{0,1:T(8,128)S(1)}, f32[512,32]{0,1:T(8,128)}, u32[]{:S(2)}) copy-start(f32[512,32]{0,1:T(8,128)} %copy-done.36) | copy-start | bytes 196612
  308.9 131.5 %reduce-scatter.8.cloned.1.call-start = ((), (), s32[]{:S(2)}) async-start(), calls=%async_computation.8 | async-start | bytes 6291456 | tf_op jit(solution)/shard_map/reduce_scatter | solution.py:337
  341.8 32.5 %copy-start.41 = (bf16[1,16,3072]{2,0,1:T(2,128)(2,1)S(1)}, bf16[1,16,3072]{2,0,1:T(2,128)(2,1)}, u32[]{:S(2)}) copy-start(bf16[1,16,3072]{2,0,1:T(2,128)(2,1)} %copy-done.40) | copy-start | bytes 294916
  342.5 33.6 %copy-start.29 = (bf16[1,512,16,64]{1,3,2,0:T(8,128)(2,1)}, bf16[1,512,16,64]{1,3,2,0:T(8,128)(2,1)S(1)}, u32[]{:S(2)}) copy-start(bf16[1,512,16,64]{1,3,2,0:T(8,128)(2,1)S(1)} %pad_maximum_fusion.4) | copy-start | bytes 3145732
  342.6 33.5 %copy-start.31 = (bf16[1,512,16,64]{1,3,2,0:T(8,128)(2,1)}, bf16[1,512,16,64]{1,3,2,0:T(8,128)(2,1)S(1)}, u32[]{:S(2)}) copy-start(bf16[1,512,16,64]{1,3,2,0:T(8,128)(2,1)S(1)} %pad_maximum_fusion.3) | copy-start | bytes 3145732
  342.6 33.5 %copy-start.12 = (bf16[1,512,1024]{2,1,0:T(8,128)(2,1)S(1)}, bf16[1,512,1024]{2,1,0:T(8,128)(2,1)}, u32[]{:S(2)}) copy-start(bf16[1,512,1024]{2,1,0:T(8,128)(2,1)} %param.27) | copy-start | bytes 3145732
  342.6 33.5 %copy-start.62 = (f32[512]{0:T(512)S(1)}, f32[512]{0:T(512)}, u32[]{:S(2)}) copy-start(f32[512]{0:T(512)} %copy-done.61) | copy-start | bytes 6148
  342.6 33.5 %copy-start.64 = (f32[512]{0:T(512)S(1)}, f32[512]{0:T(512)}, u32[]{:S(2)}) copy-start(f32[512]{0:T(512)} %copy-done.63) | copy-start | bytes 6148
  342.7 33.5 %copy-start.71 = (f32[1024]{0:T(1024)S(1)}, f32[1024]{0:T(1024)}, u32[]{:S(2)}) copy-start(f32[1024]{0:T(1024)} %param.29) | copy-start | bytes 12292
  342.7 33.5 %copy-start.78 = (f32[1024]{0:T(1024)S(1)}, f32[1024]{0:T(1024)}, u32[]{:S(2)}) copy-start(f32[1024]{0:T(1024)} %param.30) | copy-start | bytes 12292
  376.2 3.3 copy-start.54
  376.8 3.3 copy-start.21
  376.8 3.3 copy-start.52
  376.8 4.1 copy-start.18
  376.8 4.1 copy-start.60
  385.9 156.1 %all-reduce.2.cloned.1.call-start = ((), (), s32[]{:S(2)}) async-start(), calls=%async_computation.9 | async-start | bytes 4194304 | tf_op jit(solution)/shard_map/psum | solution.py:336
  440.4 159.2 %all-gather.8.cloned.1.call-start = ((), (), s32[]{:S(2)}) async-start(), calls=%async_computation.7 | async-start | bytes 6291456 | tf_op jit(solution)/shard_map/all_gather | solution.py:338
  542.0 8.3 %copy-start.6 = (f32[1,512,1024]{2,1,0:T(8,128)S(1)}, f32[1,512,1024]{2,1,0:T(8,128)}, u32[]{:S(2)}) copy-start(f32[1,512,1024]{2,1,0:T(8,128)} %copy-done.5) | copy-start | bytes 6291460
  542.0 8.3 %copy-start.45 = (bf16[1,16,1024]{2,0,1:T(2,128)(2,1)S(1)}, bf16[1,16,1024]{2,0,1:T(2,128)(2,1)}, u32[]{:S(2)}) copy-start(bf16[1,16,1024]{2,0,1:T(2,128)(2,1)} %copy-done.44) | copy-start | bytes 98308
  542.1 8.3 %copy-start.73 = (f32[1024]{0:T(1024)S(1)}, f32[1024]{0:T(1024)}, u32[]{:S(2)}) copy-start(f32[1024]{0:T(1024)} %param.46) | copy-start | bytes 12292
  553.0 6.8 %copy-start.56 = (bf16[1,16,1024]{2,0,1:T(2,128)(2,1)S(1)}, bf16[1,16,1024]{2,0,1:T(2,128)(2,1)}, u32[]{:S(2)}) copy-start(bf16[1,16,1024]{2,0,1:T(2,128)(2,1)} %copy-done.55) | copy-start | bytes 98308
  559.8 3.8 copy-start.9
  602.6 3.8 copy-start.1
  (30 other events, 59.8 us)
Sparse Core Ops, SparseCore 0:
  25.5 35.8 all-gather.5
  63.5 33.1 all-gather.3
  308.4 31.8 reduce-scatter.3
  342.4 31.8 reduce-scatter.5
  386.0 54.2 reduce-scatter.7
  444.2 97.8 all-reduce.1
  543.6 55.9 all-gather.7
where the time goes:
time: 622 us; the launch traced here: 614 us
  waiting for transfers between devices  274 us (44%)
  matrix products  227 us (36%)
  other arithmetic  47.6 us (8%)
  local copies, waits for them, and re-layouts  46.8 us (8%)
  between operations  16.4 us (3%)
    psum x1, waiting for transfers between devices, body(): summed = lax.psum(packed.astype(jnp.bfloat16), 'dp')  101 us
    reduce_scatter x1, waiting for transfers between devices, body(): lax.psum_scatter(summed, 'seq', scatter_dimension=2, tiled=True)  54.4 us
    all_gather x1, waiting for transfers between devices, body(): lax.all_gather(owned.astype(jnp.bfloat16), 'seq', axis=2, tiled=True)  32.4 us
    reduce_scatter x1, waiting for transfers between devices, body(): lax.psum_scatter(value_full.astype(jnp.bfloat16), 'seq', scatter_dimensio...  31.6 us
    reduce_scatter x1, waiting for transfers between devices, body(): lax.psum_scatter(key_full.astype(jnp.bfloat16), 'seq', scatter_dimension=...  27.5 us
    all_gather x1, waiting for transfers between devices, body(): lax.all_gather(key_low, 'seq', axis=1, tiled=True)  26.5 us
    dot_general x4, matrix products, project(): jnp.einsum('cra,cae->cre', low_rank, up_pick, preferred_element_type=jnp....  24.4 us
    dot_general x4, matrix products, project_back(): jnp.einsum('cre,de->crd', grad_low, weight, preferred_element_type=jnp.fl...  23 us
  transfers between devices with their start and end apart: 7, of which 6 were waited for; matrix products, arithmetic and copies ran while one was open for 12% of the time, Pallas kernels for 0%

commit v1 on v0

v1 whole, which is shorter than its diff:
```python
import functools

import jax
import jax.numpy as jnp
import numpy as np
from jax import lax
from jax.experimental import pallas as pl
from jax.experimental.pallas import tpu as pltpu
from jax.sharding import PartitionSpec as P

HEADS = 16
HD = 64
GRID = 16
NADAPT = 8
RANK = 16
EPSILON = 1e-06
LANES = 128
EXTRA = 48

F32 = jnp.float32
BF16 = jnp.bfloat16
NN = (((1,), (0,)), ((), ()))
NT = (((1,), (1,)), ((), ()))

ERFC = (
    0.16918800211151383,
    0.1707152747822528,
    0.14833885959986734,
    0.21492717178376733,
    -0.09465313901935662,
    0.5477232747113128,
    -0.5122807406271995,
    0.48556441585520754,
    -0.1295231387829952,
)


def dot(a, b, dims=NN):
    return lax.dot_general(a, b, dims, preferred_element_type=F32)


def params(steps=1):
    return pltpu.CompilerParams(
        dimension_semantics=("arbitrary",) * steps, vmem_limit_bytes=60 << 20
    )


def cost(flops, moved, exps=0):
    return pl.CostEstimate(flops=int(flops), bytes_accessed=int(moved), transcendentals=int(exps))


def norm_rows(values):
    centre = values - jnp.mean(values, axis=-1, keepdims=True)
    spread = lax.rsqrt(jnp.mean(centre * centre, axis=-1, keepdims=True) + EPSILON)
    return centre * spread, spread


def norm_back(grad_rows, normed, spread, gain):
    scaled = grad_rows * gain
    first = jnp.mean(scaled, axis=-1, keepdims=True)
    second = jnp.mean(scaled * normed, axis=-1, keepdims=True)
    return spread * (scaled - first - normed * second)


def rotary_tables(length):
    half = HD // 2
    side = half // 3
    lead = half - 2 * side
    token = np.arange(length)
    pair = np.arange(half)
    kind = np.where(pair < lead, 0, np.where(pair < lead + side, 1, 2))
    local = np.where(kind == 0, pair, np.where(kind == 1, pair - lead, pair - lead - side))
    total = np.where(kind == 0, lead, side)
    frequency = np.power(
        np.float32(10000.0), -local.astype(np.float32) / total.astype(np.float32)
    ).astype(np.float32)
    place = np.where(
        kind[None] == 0,
        (token // (GRID * GRID))[:, None],
        np.where(kind[None] == 1, (token // GRID % GRID)[:, None], (token % GRID)[:, None]),
    ).astype(np.float32)
    angle = place * frequency[None]
    cosine, sine = np.cos(angle), np.sin(angle)
    cos_rows = np.concatenate([cosine] * 4, axis=1).astype(np.float32)
    sin_rows = np.concatenate([-sine, sine, -sine, sine], axis=1).astype(np.float32)
    return cos_rows, sin_rows


def swap_halves(values):
    lane = lax.broadcasted_iota(jnp.int32, values.shape, 1)
    low = lax.rem(lane, HD) < HD // 2
    return jnp.where(
        low, pltpu.roll(values, LANES - HD // 2, 1), pltpu.roll(values, HD // 2, 1)
    )


def head_mask(values, head):
    lane = lax.broadcasted_iota(jnp.int32, (1, LANES), 1)
    keep = (lane < HD) if head == 0 else (lane >= HD)
    return jnp.where(keep, values, jnp.zeros_like(values))


def whole(shape):
    return pl.BlockSpec(shape, lambda *_: (0,) * len(shape))


def chosen(shape):
    return pl.BlockSpec((1,) + shape, lambda j, at: (at[0], 0, 0))


def qkv_kernel(at, x, gain, shift, w, bias, down, up, cos, sin, qkv, low, h1, *, tile, width):
    j = pl.program_id(0)

    @pl.when(j == 0)
    def _():
        normed, _s = norm_rows(x[...].astype(F32))
        rows = (normed * gain[...] + shift[...]).astype(BF16)
        h1[...] = rows
        low[...] = dot(rows, down[0], NT).astype(BF16)

    out = dot(h1[...], w[...]) + bias[...] + dot(low[...], up[0])
    rotated = 2 * width // tile

    @pl.when(j < rotated)
    def _():
        scale = jnp.where(j < rotated // 2, HD**-0.5, 1.0).astype(F32)
        c = cos[...] * scale
        s = sin[...] * scale
        for g in range(tile // LANES):
            part = out[:, g * LANES : (g + 1) * LANES]
            qkv[:, g * LANES : (g + 1) * LANES] = (part * c + swap_halves(part) * s).astype(BF16)

    @pl.when(j >= rotated)
    def _():
        qkv[...] = out.astype(BF16)


def qkv_rows(at, x, gain, shift, w, bias, down, up, cos, sin):
    rows, width = x.shape
    cols = w.shape[1]
    tile = 512
    return pl.pallas_call(
        functools.partial(qkv_kernel, tile=tile, width=width),
        grid_spec=pltpu.PrefetchScalarGridSpec(
            num_scalar_prefetch=1,
            grid=(cols // tile,),
            in_specs=[
                whole((rows, width)),
                whole((1, width)),
                whole((1, width)),
                pl.BlockSpec((width, tile), lambda j, at: (0, j)),
                pl.BlockSpec((1, tile), lambda j, at: (0, j)),
                chosen((RANK, width)),
                pl.BlockSpec((1, RANK, tile), lambda j, at: (at[0], 0, j)),
                whole((rows, LANES)),
                whole((rows, LANES)),
            ],
            out_specs=[
                pl.BlockSpec((rows, tile), lambda j, at: (0, j)),
                whole((rows, RANK)),
            ],
            scratch_shapes=[pltpu.VMEM((rows, width), BF16)],
        ),
        out_shape=[
            jax.ShapeDtypeStruct((rows, cols), BF16),
            jax.ShapeDtypeStruct((rows, RANK), BF16),
        ],
        compiler_params=params(),
        cost_estimate=cost(2 * rows * width * cols, 2 * width * cols + 2 * rows * (width + cols)),
        name="qkv_rows",
    )(at, x, gain, shift, w, bias, down, up, cos, sin)


def attend_kernel(q, k0, v0, k1, v1, out, lse):
    i = pl.program_id(0)
    rows, wide = q.shape
    keys = jnp.concatenate([k0[...], k1[...]], axis=0)
    values_t = jnp.concatenate([v0[...], v1[...]], axis=0).T

    def scores(item):
        pair, head = item
        cut = slice(pair * LANES, (pair + 1) * LANES)
        return dot(keys[:, cut], head_mask(q[:, cut], head), NT)

    items = [(pair, head) for pair in range(wide // LANES) for head in range(2)]
    held = []
    now = scores(items[0])
    for n, (pair, head) in enumerate(items):
        later = scores(items[n + 1]) if n + 1 < len(items) else None
        top = jnp.max(now, axis=0, keepdims=True)
        weights = jnp.exp(now - top)
        total = jnp.sum(weights, axis=0, keepdims=True)
        first = pair * LANES + head * HD
        mixed = dot(values_t[first : first + HD], weights.astype(BF16))
        held.append(mixed * (1.0 / total))
        lse[pl.ds(i * (wide // HD) + n, 1), :] = top + jnp.log(total)
        if head == 1:
            both = jnp.concatenate(held, axis=0).T
            out[:, pair * LANES : (pair + 1) * LANES] = both.astype(BF16)
            held = []
        now = later


def attend(own, peer):
    rows = own.shape[0]
    width = own.shape[1] // 3
    others = peer.shape[0]
    wide = 2 * LANES
    steps = width // wide

    def part(count, which):
        return pl.BlockSpec((count, wide), lambda i: (0, i + which * steps))

    return pl.pallas_call(
        attend_kernel,
        grid=(steps,),
        in_specs=[part(rows, 0), part(rows, 1), part(rows, 2), part(others, 1), part(others, 2)],
        out_specs=[
            pl.BlockSpec((rows, wide), lambda i: (0, i)),
            whole((HEADS, rows)),
        ],
        out_shape=[
            jax.ShapeDtypeStruct((rows, width), BF16),
            jax.ShapeDtypeStruct((HEADS, rows), F32),
        ],
        compiler_params=params(),
        cost_estimate=cost(
            16 * rows * (rows + others) * width, 4 * width * (rows + others), rows * HEADS * others
        ),
        name="attend",
    )(own, own, own, peer, peer)


def gelu_both(f):
    z = jnp.abs(f) * (0.5**0.5)
    t = 1.0 / (1.0 + 0.3 * z)
    poly = ERFC[-1]
    for c in ERFC[-2::-1]:
        poly = poly * t + c
    bell = jnp.exp(f * f * -0.5)
    tail = (0.5 * poly) * t * bell
    phi = jnp.where(f < 0, tail, 1.0 - tail)
    return f * phi, phi + f * (bell * 0.3989422804014327)


def put_pieces(ref, slot, first, tile, code, spread):
    for p in range(tile.shape[1] // LANES):
        ref[(first + p) ^ code, slot] = tile[:, p * LANES : (p + 1) * LANES].astype(BF16)


def block_kernel(
    at,
    x, o, cot, lse, w_out, b_out, out_down, out_up, gain, shift,
    w1, b1, down1, up1, w2, b2, down2, up2,
    y_out, dx1_out, go_out, delta_out, pieces,
    x1, h2, y, dh2, low_o, low1, low1_t, grad2, grad2_t, low2, grad1,
    *, tile,
):
    j = pl.program_id(0)
    last = pl.num_programs(0) - 1
    code = at[1]
    rows, width = x.shape

    @pl.when(j == 0)
    def _():
        low = dot(o[...], out_down[0], NT).astype(BF16)
        low_o[...] = low
        mid = x[...].astype(F32) + (dot(o[...], w_out[...]) + b_out[...] + dot(low, out_up[0]))
        x1[...] = mid
        normed, _s = norm_rows(mid)
        rows2 = (normed * gain[...] + shift[...]).astype(BF16)
        h2[...] = rows2
        low_1 = dot(rows2, down1[0], NT).astype(BF16)
        low1[...] = low_1
        low1_t[...] = low_1.T
        g2 = dot(cot[...], up2[0], NT).astype(BF16)
        grad2[...] = g2
        grad2_t[...] = g2.T
        y[...] = jnp.zeros_like(y)
        dh2[...] = jnp.zeros_like(dh2)
        low2[...] = jnp.zeros_like(low2)
        grad1[...] = jnp.zeros_like(grad1)

    f = dot(h2[...], w1[...]) + b1[...] + dot(low1[...], up1[0])
    back = dot(cot[...], w2[...], NT) + dot(grad2[...], down2[0])
    act, slope = gelu_both(f)
    act = act.astype(BF16)
    df = (back * slope).astype(BF16)
    y[...] += dot(act, w2[...])
    dh2[...] += dot(df, w1[...], NT)
    low2[...] += dot(act, down2[0], NT)
    grad1[...] += dot(df, up1[0], NT)
    first = j * (tile // LANES)
    up1_grad = dot(low1_t[...], df)
    down2_grad = dot(grad2_t[...], act)
    for p in range(tile // LANES):
        cut = slice(p * LANES, (p + 1) * LANES)
        pieces[(first + p) ^ code, 0] = up1_grad[:, cut].astype(BF16)
        pieces[(first + p) ^ code, 1] = down2_grad[:, cut].astype(BF16)

    @pl.when(j == last)
    def _():
        low_2 = low2[...].astype(BF16)
        total = x1[...] + (y[...] + b2[...] + dot(low_2, up2[0]))
        y_out[...] = total.astype(BF16)
        up2_grad = dot(low_2.T, cot[...])
        g1 = grad1[...].astype(BF16)
        back2 = dh2[...] + dot(g1, down1[0])
        down1_grad = dot(g1.T, h2[...])
        normed, spread = norm_rows(x1[...])
        dx1 = cot[...].astype(F32) + norm_back(back2, normed, spread, gain[...])
        dx1_out[...] = dx1
        da = dx1.astype(BF16)
        g_o = dot(da, out_up[0], NT).astype(BF16)
        go = (dot(da, w_out[...], NT) + dot(g_o, out_down[0])).astype(BF16)
        go_out[EXTRA : EXTRA + rows, :] = go
        up_o_grad = dot(low_o[...].T, da)
        down_o_grad = dot(g_o.T, o[...])
        for slot, grad in enumerate((up2_grad, down1_grad, up_o_grad, down_o_grad)):
            for p in range(width // LANES):
                cut = slice(p * LANES, (p + 1) * LANES)
                pieces[(slot * (width // LANES) + p) ^ code, 2] = grad[:, cut].astype(BF16)
        product = go.astype(F32) * o[...].astype(F32)
        high = product.astype(BF16)
        rest = (product - high.astype(F32)).astype(BF16)
        lane = lax.broadcasted_iota(jnp.int32, (HEADS, width), 1)
        head = lax.broadcasted_iota(jnp.int32, (HEADS, width), 0)
        pick = (lane // HD == head).astype(BF16)
        delta = dot(pick, high, NT) + dot(pick, rest, NT)
        delta_out[...] = delta
        if rows < width // 2:
            go_out[0:EXTRA, :] = jnp.zeros((EXTRA, width), BF16)
        for side, stat in enumerate((lse[...], delta)):
            left = stat
            for n in range(3):
                part = left.astype(BF16)
                go_out[16 * n : 16 * n + 16, side * (width // 2) : side * (width // 2) + rows] = part
                left = left - part.astype(F32)


def block_rows(at, x, o, cot, lse, out_set, norm_set, fc1_set, fc2_set, groups):
    rows, width = x.shape
    w_out, b_out, out_down, out_up = out_set
    w1, b1, down1, up1 = fc1_set
    w2, b2, down2, up2 = fc2_set
    ff = w1.shape[1]
    tile = 512
    row_block = whole((rows, width))
    return pl.pallas_call(
        functools.partial(block_kernel, tile=tile),
        grid_spec=pltpu.PrefetchScalarGridSpec(
            num_scalar_prefetch=1,
            grid=(ff // tile,),
            in_specs=[
                row_block,
                row_block,
                row_block,
                whole((HEADS, rows)),
                whole((width, width)),
                whole((1, width)),
                chosen((RANK, width)),
                chosen((RANK, width)),
                whole((1, width)),
                whole((1, width)),
                pl.BlockSpec((width, tile), lambda j, at: (0, j)),
                pl.BlockSpec((1, tile), lambda j, at: (0, j)),
                chosen((RANK, width)),
                pl.BlockSpec((1, RANK, tile), lambda j, at: (at[0], 0, j)),
                pl.BlockSpec((tile, width), lambda j, at: (j, 0)),
                whole((1, width)),
                pl.BlockSpec((1, RANK, tile), lambda j, at: (at[0], 0, j)),
                chosen((RANK, width)),
            ],
            out_specs=[
                row_block,
                row_block,
                whole((EXTRA + rows, width)),
                whole((HEADS, rows)),
                whole((groups, 3, RANK, LANES)),
            ],
            scratch_shapes=[
                pltpu.VMEM((rows, width), F32),
                pltpu.VMEM((rows, width), BF16),
                pltpu.VMEM((rows, width), F32),
                pltpu.VMEM((rows, width), F32),
                pltpu.VMEM((rows, RANK), BF16),
                pltpu.VMEM((rows, RANK), BF16),
                pltpu.VMEM((RANK, rows), BF16),
                pltpu.VMEM((rows, RANK), BF16),
                pltpu.VMEM((RANK, rows), BF16),
                pltpu.VMEM((rows, RANK), F32),
                pltpu.VMEM((rows, RANK), F32),
            ],
        ),
        out_shape=[
            jax.ShapeDtypeStruct((rows, width), BF16),
            jax.ShapeDtypeStruct((rows, width), F32),
            jax.ShapeDtypeStruct((EXTRA + rows, width), BF16),
            jax.ShapeDtypeStruct((HEADS, rows), F32),
            jax.ShapeDtypeStruct((groups, 3, RANK, LANES), BF16),
        ],
        compiler_params=params(),
        cost_estimate=cost(
            8 * rows * width * ff + 4 * rows * width * width, 4 * width * ff, rows * ff
        ),
        name="block_rows",
    )(
        at, x, o, cot, lse, w_out, b_out, out_down, out_up, *norm_set,
        w1, b1, down1, up1, w2, b2, down2, up2,
    )


def attend_back_kernel(
    q0, k0, v0, q1, k1, v1, go, gp, stats, lse0, delta0, cos, sin, out, lse1, delta1
):
    i = pl.program_id(0)
    rows = q0.shape[0]
    peers = gp.shape[0]
    half = stats.shape[2] // 2

    @pl.when(i == 0)
    def _():
        for n in range(peers):
            for side, ref in enumerate((lse1, delta1)):
                cut = slice(side * half, side * half + rows)
                ref[n] = (
                    stats[n, 0:16, cut].astype(F32)
                    + stats[n, 16:32, cut].astype(F32)
                    + stats[n, 32:48, cut].astype(F32)
                )

    keys = jnp.concatenate([k0[...], k1[...]], axis=0)
    values = jnp.concatenate([v0[...], v1[...]], axis=0)
    keys_t = keys.T

    def first(item):
        head, peer = item
        if peer is None:
            q = head_mask(q0[...], head)
            g = head_mask(go[EXTRA : EXTRA + rows, :], head)
            return dot(keys, q, NT), dot(values, g, NT), q, g
        q = head_mask(q1[peer * rows : (peer + 1) * rows, :], head)
        g = head_mask(gp[peer, EXTRA : EXTRA + rows, :], head)
        return dot(k0[...], q, NT), dot(v0[...], g, NT), q, g

    items = [(head, None) for head in range(2)]
    items += [(head, peer) for peer in range(peers) for head in range(2)]
    grad_k = grad_v = None
    grad_q = []
    now = first(items[0])
    for n, (head, peer) in enumerate(items):
        later = first(items[n + 1]) if n + 1 < len(items) else None
        s, dp, q, g = now
        row = pl.ds(2 * i + head, 1)
        lse = lse0[row, :] if peer is None else lse1[peer, row, :]
        delta = delta0[row, :] if peer is None else delta1[peer, row, :]
        prob = jnp.exp(s - lse)
        ds = (prob * (dp - delta)).astype(BF16)
        prob = prob.astype(BF16)
        if peer is None:
            grad_q.append(dot(keys_t[head * HD : (head + 1) * HD], ds))
        more_v = dot(prob[:rows], g)
        more_k = dot(ds[:rows], q)
        grad_v = more_v if grad_v is None else grad_v + more_v
        grad_k = more_k if grad_k is None else grad_k + more_k
        now = later

    def unrotate(values):
        return values * cos[...] - swap_halves(values) * sin[...]

    out[0] = unrotate(jnp.concatenate(grad_q, axis=0).T * (HD**-0.5)).astype(BF16)
    out[1] = unrotate(grad_k).astype(BF16)
    out[2] = grad_v.astype(BF16)


def attend_back(own, peer, go, gp, lse, delta, cos, sin):
    rows = own.shape[0]
    width = own.shape[1] // 3
    others = peer.shape[0]
    peers = gp.shape[0]
    steps = width // LANES

    def part(count, which):
        return pl.BlockSpec((count, LANES), lambda i: (0, i + which * steps))

    return pl.pallas_call(
        attend_back_kernel,
        grid=(steps,),
        in_specs=[
            part(rows, 0), part(rows, 1), part(rows, 2),
            part(others, 0), part(others, 1), part(others, 2),
            part(rows + EXTRA, 0),
            pl.BlockSpec((peers, rows + EXTRA, LANES), lambda i: (0, 0, i)),
            whole((peers, EXTRA, width)),
            whole((HEADS, rows)),
            whole((HEADS, rows)),
            whole((rows, LANES)),
            whole((rows, LANES)),
        ],
        out_specs=pl.BlockSpec((3, rows, LANES), lambda i: (0, 0, i)),
        out_shape=jax.ShapeDtypeStruct((3, rows, width), BF16),
        scratch_shapes=[
            pltpu.VMEM((peers, HEADS, rows), F32),
            pltpu.VMEM((peers, HEADS, rows), F32),
        ],
        compiler_params=params(),
        cost_estimate=cost(
            12 * 2 * rows * (rows + others) * width, 8 * width * (rows + others), rows * others
        ),
        name="attend_back",
    )(own, own, own, peer, peer, peer, go, gp, gp, lse, delta, cos, sin)


def qkv_grad_kernel(at, g, low, x, gain, shift, up, pieces, rank_grad):
    code = at[1]
    width = x.shape[1]
    low_t = low[...].T
    total = None
    for n in range(3):
        grad = dot(low_t, g[n])
        for p in range(width // LANES):
            piece = n * (width // LANES) + p
            pieces[piece ^ code, 0] = grad[:, p * LANES : (p + 1) * LANES].astype(BF16)
        more = dot(g[n], up[0, :, n * width : (n + 1) * width], NT)
        total = more if total is None else total + more
    rank = total.astype(BF16)
    rank_grad[...] = rank
    normed, _s = norm_rows(x[...].astype(F32))
    h1 = (normed * gain[...] + shift[...]).astype(BF16)
    grad = dot(rank.T, h1)
    for p in range(width // LANES):
        piece = 3 * (width // LANES) + p
        pieces[piece ^ code, 0] = grad[:, p * LANES : (p + 1) * LANES].astype(BF16)


def qkv_grad(at, g, low, x, gain, shift, up, groups):
    rows, width = x.shape
    return pl.pallas_call(
        qkv_grad_kernel,
        grid_spec=pltpu.PrefetchScalarGridSpec(
            num_scalar_prefetch=1,
            grid=(1,),
            in_specs=[
                whole((3, rows, width)),
                whole((rows, RANK)),
                whole((rows, width)),
                whole((1, width)),
                whole((1, width)),
                chosen((RANK, 3 * width)),
            ],
            out_specs=[whole((groups, 1, RANK, LANES)), whole((rows, RANK))],
        ),
        out_shape=[
            jax.ShapeDtypeStruct((groups, 1, RANK, LANES), BF16),
            jax.ShapeDtypeStruct((rows, RANK), BF16),
        ],
        compiler_params=params(),
        cost_estimate=cost(2 * rows * 16 * 3 * width * 4, 8 * rows * width),
        name="qkv_grad",
    )(at, g, low, x, gain, shift, up)


def input_grad_kernel(at, g, w, rank_grad, down, x, gain, dx1, out, total):
    j = pl.program_id(0)

    @pl.when(j == 0)
    def _():
        total[...] = dot(rank_grad[...], down[0])

    total[...] += dot(g[0], w[...], NT)

    @pl.when(j == pl.num_programs(0) - 1)
    def _():
        normed, spread = norm_rows(x[...].astype(F32))
        out[...] = dx1[...] + norm_back(total[...], normed, spread, gain[...])


def input_grad(at, g, w, rank_grad, down, x, gain, dx1):
    rows, width = x.shape
    tile = 512
    per = width // tile
    return pl.pallas_call(
        input_grad_kernel,
        grid_spec=pltpu.PrefetchScalarGridSpec(
            num_scalar_prefetch=1,
            grid=(3 * per,),
            in_specs=[
                pl.BlockSpec((1, rows, tile), lambda j, at: (j // per, 0, j % per)),
                pl.BlockSpec((width, tile), lambda j, at: (0, j)),
                whole((rows, RANK)),
                chosen((RANK, width)),
                whole((rows, width)),
                whole((1, width)),
                whole((rows, width)),
            ],
            out_specs=whole((rows, width)),
            scratch_shapes=[pltpu.VMEM((rows, width), F32)],
        ),
        out_shape=jax.ShapeDtypeStruct((rows, width), F32),
        compiler_params=params(),
        cost_estimate=cost(6 * rows * width * width, 6 * width * width + 16 * rows * width),
        name="input_grad",
    )(at, g, w, rank_grad, down, x, gain, dx1)


def flip(values, axis, bit):
    size = lax.axis_size(axis)
    return lax.ppermute(values, axis, [(n, n ^ bit) for n in range(size)])


def swap_order(groups):
    bits = [("dp", 1)]
    n = 1
    while n < lax.axis_size("seq"):
        bits.append(("seq", n))
        n *= 2
    n = 2
    while n < lax.axis_size("dp"):
        bits.append(("dp", n))
        n *= 2
    count = groups.bit_length() - 1
    return bits[:count], bits[count:]


def place_code(groups):
    halves, _rest = swap_order(groups)
    code = jnp.int32(0)
    for n, (axis, bit) in enumerate(halves):
        on = (lax.axis_index(axis) & bit) != 0
        code = code + jnp.where(on, groups >> (n + 1), 0).astype(jnp.int32)
    return code


def sum_pieces(pieces, index_all, groups):
    halves, rest = swap_order(groups)
    held = pieces[None]
    slots = [0]
    for axis, bit in halves:
        half = held.shape[1] // 2
        arrived = flip(held[:, half:], axis, bit)
        kept = held[:, :half]
        if axis == "seq":
            held = (kept.astype(F32) + arrived.astype(F32)).astype(BF16)
        else:
            held = jnp.concatenate([kept, arrived], axis=0)
            slots = slots + [slot ^ bit for slot in slots]
    place = lax.axis_index("dp")
    owners = jnp.stack([index_all[place ^ slot] for slot in slots])
    onehot = (jnp.arange(NADAPT, dtype=jnp.int32)[:, None] == owners[None, :]).astype(F32)
    total = jnp.sum(
        onehot[:, :, None, None, None, None] * held.astype(F32)[None], axis=1
    )
    total = jnp.transpose(total, (1, 2, 0, 3, 4)).astype(BF16)
    for axis, bit in rest:
        total = (total.astype(F32) + flip(total, axis, bit).astype(F32)).astype(BF16)
    for axis, bit in halves[::-1]:
        total = jnp.concatenate([total, flip(total, axis, bit)], axis=0)
    return total


def spread_kernel(at, pieces, *outs, plan):
    code = at[1]
    for ref, part, first, count in zip(outs, *plan):
        for p in range(count):
            ref[:, :, p * LANES : (p + 1) * LANES] = pieces[(first + p) ^ code, part].astype(F32)


def spread(at, pieces, plan):
    parts, firsts, counts = plan
    shapes = [(NADAPT, RANK, count * LANES) for count in counts]
    return pl.pallas_call(
        functools.partial(spread_kernel, plan=plan),
        grid_spec=pltpu.PrefetchScalarGridSpec(
            num_scalar_prefetch=1,
            grid=(1,),
            in_specs=[whole(pieces.shape)],
            out_specs=[whole(shape) for shape in shapes],
        ),
        out_shape=[jax.ShapeDtypeStruct(shape, F32) for shape in shapes],
        compiler_params=params(),
        cost_estimate=cost(1, 6 * pieces.size),
        name="spread",
    )(at, pieces)


def body(
    clip_tokens, adapter_index, ln1_gain, ln1_bias, qkv_weight, qkv_bias, qkv_down, qkv_up,
    out_weight, out_bias, out_down, out_up, ln2_gain, ln2_bias, fc1_weight, fc1_bias, fc1_down,
    fc1_up, fc2_weight, fc2_bias, fc2_down, fc2_up, cotangent,
):
    _one, rows, width = clip_tokens.shape
    devices = lax.axis_size("seq")
    here = lax.axis_index("seq")
    groups = 32
    row = lambda v: v.reshape(1, -1)
    x = clip_tokens[0]
    cot = cotangent[0]
    at = jnp.stack([adapter_index[0], place_code(groups)])
    index_all = lax.all_gather(adapter_index, "dp", axis=0, tiled=True)

    def from_peer(values, shift):
        return lax.ppermute(
            values, "seq", [((n + shift) % devices, n) for n in range(devices)]
        )

    cos_all, sin_all = (jnp.asarray(t) for t in rotary_tables(rows * devices))

    def tables(place):
        return tuple(
            lax.dynamic_slice_in_dim(t, place * rows, rows, 0) for t in (cos_all, sin_all)
        )

    cos, sin = tables(here)
    peers = range(1, devices)
    x_peer = jnp.concatenate([from_peer(x, n) for n in peers], axis=0)
    peer_tables = [tables((here + n) % devices) for n in peers]
    cos_peer = jnp.concatenate([t[0] for t in peer_tables], axis=0)
    sin_peer = jnp.concatenate([t[1] for t in peer_tables], axis=0)
    first_set = (row(ln1_gain), row(ln1_bias), qkv_weight, row(qkv_bias), qkv_down, qkv_up)
    own, low_qkv = qkv_rows(at, x, *first_set, cos, sin)
    peer, _low = qkv_rows(at, x_peer, *first_set, cos_peer, sin_peer)
    mixed, lse = attend(own, peer)
    block_output, dx1, go, delta, pieces_a = block_rows(
        at, x, mixed, cot, lse,
        (out_weight, row(out_bias), out_down, out_up),
        (row(ln2_gain), row(ln2_bias)),
        (fc1_weight, row(fc1_bias), fc1_down, fc1_up),
        (fc2_weight, row(fc2_bias), fc2_down, fc2_up),
        groups,
    )
    go_peer = jnp.stack([from_peer(go, n) for n in peers])
    grad_qkv = attend_back(own, peer, go, go_peer, lse, delta, cos, sin)
    pieces_b, rank_grad = qkv_grad(
        at, grad_qkv, low_qkv, x, row(ln1_gain), row(ln1_bias), qkv_up, groups
    )
    grad_in = input_grad(at, grad_qkv, qkv_weight, rank_grad, qkv_down, x, row(ln1_gain), dx1)
    sums_a = sum_pieces(pieces_a, index_all, groups)
    sums_b = sum_pieces(pieces_b, index_all, groups)
    per = width // LANES
    up1, down2, up2, down1, up_o, down_o = spread(
        at, sums_a, ((0, 1, 2, 2, 2, 2), (0, 0, 0, per, 2 * per, 3 * per), (32, 32, per, per, per, per))
    )
    up_qkv, down_qkv = spread(at, sums_b, ((0, 0), (0, 3 * per), (3 * per, per)))
    return (
        block_output[None], grad_in[None], down_qkv, up_qkv, down_o, up_o, down1, up1, down2, up2,
    )


def solution(mesh):
    split = P("dp", "seq", None)
    return jax.shard_map(
        body,
        mesh=mesh,
        in_specs=(split, P("dp")) + (P(),) * 20 + (split,),
        out_specs=(split, split) + (P(),) * 8,
        check_vma=False,
    )
```

time: 622 us -> 267 us (0.43); the launches traced: 614 us -> 266 us
  matrix products: 227 us -> 0 us
  waiting for transfers between devices: 274 us -> 67.3 us
  Pallas kernels: 0 us -> 143 us
  other arithmetic: 47.6 us -> 1.5 us
  local copies, waits for them, and re-layouts: 46.8 us -> 21.7 us
  starting transfers between devices: 0.83 us -> 20.6 us
  between operations: 16.4 us -> 1.58 us
  blocking collectives: 0 us -> 11.2 us
    dot_general x54 -> x0, matrix products: 227 us -> none  [the longest x4 24.4 us: project(): jnp.einsum('cra,cae->cre', low_rank, up_pick, preferred_element_type=jnp....]
    pallas_call x0 -> x9, Pallas kernels: none -> 143 us  [the longest x1 44.9 us: block_rows(): pl.pallas_call(functools.partial(block_kernel, tile=tile), grid_spec=pltp...]
    reduce_scatter x3 -> x0, waiting for transfers between devices: 114 us -> none  [the longest x1 54.4 us: body(): lax.psum_scatter(summed, 'seq', scatter_dimension=2, tiled=True)]
    psum x1 -> x0, waiting for transfers between devices: 101 us -> none  [body(): summed = lax.psum(packed.astype(jnp.bfloat16), 'dp')]
    ppermute x0 -> x22, waiting for transfers between devices: none -> 67.3 us  [the longest x20 60.1 us: flip(): return lax.ppermute(values, axis, [(n, n ^ bit) for n in range(size)])]
    all_gather x3 -> x0, waiting for transfers between devices: 58.9 us -> none  [the longest x1 32.4 us: body(): lax.all_gather(owned.astype(jnp.bfloat16), 'seq', axis=2, tiled=True)]
    reduce_sum x8 -> x2, other arithmetic: 26.4 us -> 0.5 us  [sum_pieces(): jnp.sum(onehot[:, :, None, None, None, None] * held.astype(F32)[None], ax...]
    ppermute x0 -> x22, starting transfers between devices: none -> 20.6 us  [the longest x20 16.1 us: flip(): return lax.ppermute(values, axis, [(n, n ^ bit) for n in range(size)])]
  transfers between devices with their start and end apart: 7 -> 22, of which waited for: 6 -> 16; matrix products, arithmetic and copies ran while one was open for 12% -> 7% of each run, Pallas kernels for 0% -> 18%
where the time goes in v1:
time: 267 us; the launch traced here: 266 us
  Pallas kernels  143 us (54%)
  waiting for transfers between devices  67.3 us (25%)
  local copies, waits for them, and re-layouts  21.7 us (8%)
  starting transfers between devices  20.6 us (8%)
  blocking collectives  11.2 us (4%)
    ppermute x20, waiting for transfers between devices, flip(): return lax.ppermute(values, axis, [(n, n ^ bit) for n in range(size)])  60.1 us
    pallas_call x1, Pallas kernels, block_rows(): pl.pallas_call(functools.partial(block_kernel, tile=tile), grid_spec=pltp...  44.9 us
    pallas_call x1, Pallas kernels, attend_back(): pl.pallas_call(attend_back_kernel, grid=(steps,), in_specs=[part(rows, 0)...  30.8 us
    pallas_call x2, Pallas kernels, qkv_rows(): pl.pallas_call(functools.partial(qkv_kernel, tile=tile, width=width), gri...  25.4 us
    ppermute x20, starting transfers between devices, flip(): return lax.ppermute(values, axis, [(n, n ^ bit) for n in range(size)])  16.1 us
    pallas_call x1, Pallas kernels, attend(): pl.pallas_call(attend_kernel, grid=(steps,), in_specs=[part(rows, 0), par...  14.1 us
    pallas_call x1, Pallas kernels, input_grad(): pl.pallas_call(input_grad_kernel, grid_spec=pltpu.PrefetchScalarGridSpec(...  12.7 us
    unnamed x1, blocking collectives  11.2 us
  transfers between devices with their start and end apart: 22, of which 16 were waited for; matrix products, arithmetic and copies ran while one was open for 7% of the time, Pallas kernels for 18%

profile of v1, /device:TPU:0, one launch (start us, length us, event | category | flops | bytes accessed | tf_op | source)
XLA Modules:
  0.0 266.3 jit_solution(11874264747671658600)
XLA Ops:
  0.6 3.0 %collective-permute-start = (bf16[512,1024]{1,0:T(8,128)(2,1)}, bf16[512,1024]{1,0:T(8,128)(2,1)S(1)}, u32[]{:S(2)}, u32[]{:S(2)}) collective-permute-start(bf16[512,1024]{1,0:T(8,128)(2,1)} %bitcast.36), channel_id=1, source_target_pairs={{1,0},{0,1},{3,2},{2,3},{5,4},{4,5},{7,6},{6,7},{9,8},{8,9},{11,10... | collective-permute-start | bytes 3145736 | tf_op jit(solution)/shard_map/ppermute | solution.py:702
  4.3 0.6 pad_add_fusion.at
  4.9 2.2 constant_dynamic-slice_fusion
  7.1 12.7 %qkv_rows.2 = (bf16[512,3072]{1,0:T(8,128)(2,1)}, bf16[512,16]{1,0:T(8,128)(2,1)}) custom-call(s32[2]{0:T(128)} %pad_add_fusion.at, bf16[512,1024]{1,0:T(8,128)(2,1)} %bitcast.37, f32[1,1024]{1,0:T(1,128)} %bitcast.50, f32[1,1024]{1,0:T(1,128)} %bitcast.54, bf16[1024,3072]{1,0:T(8,128)(2,1)} %w.5, f32[1,3072]{1,0:T(1,128)} %bitcast.61, ...), custom_call_target="tpu_custom_call" | custom-call | flops 3221225472 | bytes 10485760 | tf_op jit(solution)/shard_map/qkv_rows/pallas_call | solution.py:142
  19.8 7.2 %collective-permute-done.x = bf16[512,1024]{1,0:T(8,128)(2,1)S(1)} collective-permute-done((bf16[512,1024]{1,0:T(8,128)(2,1)}, bf16[512,1024]{1,0:T(8,128)(2,1)S(1)}, u32[]{:S(2)}, u32[]{:S(2)}) %collective-permute-start) | collective-permute-done | bytes 1048608 | tf_op jit(solution)/shard_map/ppermute | solution.py:702
  27.0 1.0 copy-done.4
  28.0 12.7 %qkv_rows.3 = (bf16[512,3072]{1,0:T(8,128)(2,1)}, bf16[512,16]{1,0:T(8,128)(2,1)}) custom-call(s32[2]{0:T(128)} %pad_add_fusion.at, bf16[512,1024]{1,0:T(8,128)(2,1)} %copy-done.4, f32[1,1024]{1,0:T(1,128)} %bitcast.51, f32[1,1024]{1,0:T(1,128)} %bitcast.55, bf16[1024,3072]{1,0:T(8,128)(2,1)} %w.5, f32[1,3072]{1,0:T(1,128)} %bitcast.62, ...), custom_call_target="tpu_custom_call" | custom-call | flops 3221225472 | bytes 10485760 | tf_op jit(solution)/shard_map/qkv_rows/pallas_call | solution.py:142
  40.6 14.1 %attend.1 = (bf16[512,1024]{1,0:T(8,128)(2,1)}, f32[16,512]{1,0:T(8,128)}) custom-call(bf16[512,3072]{1,0:T(8,128)(2,1)} %get-tuple-element.30.q.k0.v0.q0, bf16[512,3072]{1,0:T(8,128)(2,1)} %get-tuple-element.30.q.k0.v0.q0, bf16[512,3072]{1,0:T(8,128)(2,1)} %get-tuple-element.30.q.k0.v0.q0, bf16[512,3072]{1,0:T(8,128)(2,1)} %get-tuple-element.31.k1.v1.q1, ...), custom_call_target="tpu_custom_call" | custom-call | flops 8589934592 | bytes 4194304 | tf_op jit(solution)/shard_map/attend/pallas_call | solution.py:214
  54.8 44.9 %block_rows.1 = (bf16[512,1024]{1,0:T(8,128)(2,1)}, f32[512,1024]{1,0:T(8,128)}, bf16[560,1024]{1,0:T(8,128)(2,1)}, f32[16,512]{1,0:T(8,128)}, bf16[32,3,16,128]{3,2,1,0:T(8,128)(2,1)}) custom-call(s32[2]{0:T(128)} %pad_add_fusion.at, bf16[512,1024]{1,0:T(8,128)(2,1)} %bitcast.38, bf16[512,1024]{1,0:T(8,128)(2,1)} %get-tuple-element.32.o, ...), custom_call_target="tpu_custom_call" | custom-call | flops 19327352832 | bytes 16777216 | tf_op jit(solution)/shard_map/block_rows/pallas_call | solution.py:349
  99.7 1.0 fusion.11
  100.8 1.4 collective-permute-done.12
  102.2 1.8 collective-permute-start.13
  104.1 5.2 %collective-permute-done.13 = bf16[2,8,3,16,128]{4,3,2,1,0:T(8,128)(2,1)S(1)} collective-permute-done((bf16[2,8,3,16,128]{4,3,2,1,0:T(8,128)(2,1)S(1)}, bf16[2,8,3,16,128]{4,3,2,1,0:T(8,128)(2,1)S(1)}, u32[]{:S(2)}, u32[]{:S(2)}) %collective-permute-start.13) | collective-permute-done | bytes 196640 | tf_op jit(solution)/shard_map/ppermute | solution.py:608
  109.3 1.8 collective-permute-start.14
  111.2 2.9 %collective-permute-done.14 = bf16[2,4,3,16,128]{4,3,2,1,0:T(8,128)(2,1)S(1)} collective-permute-done((bf16[2,4,3,16,128]{4,3,2,1,0:T(8,128)(2,1)S(1)}, bf16[2,4,3,16,128]{4,3,2,1,0:T(8,128)(2,1)S(1)}, u32[]{:S(2)}, u32[]{:S(2)}) %collective-permute-start.14) | collective-permute-done | bytes 98336 | tf_op jit(solution)/shard_map/ppermute | solution.py:608
  114.0 1.9 collective-permute-start.15
  115.9 1.5 collective-permute-start.1
  117.4 0.6 dynamic-slice
  118.0 0.8 dynamic-update-slice
  118.8 11.2 %all-reduce = s32[16]{0:T(128)S(1)} all-reduce(s32[16]{0:T(128)S(1)} %dynamic-update-slice), channel_id=1, replica_groups=mesh['dp'=16,'seq'=2] {'dp'}, use_global_device_ids=true, to_apply=%add | all-reduce | flops 16 | bytes 128
  129.9 0.7 fusion.15
  130.6 10.3 %stack.16 = s32[16]{0:T(128)S(1)} concatenate(s32[1]{0:T(128)} %get-tuple-element.105, s32[1]{0:T(128)} %get-tuple-element.104, s32[1]{0:T(128)} %get-tuple-element.103, s32[1]{0:T(128)} %get-tuple-element.102, s32[1]{0:T(128)} %get-tuple-element.101, s32[1]{0:T(128)} %get-tuple-element.100, s32[1]{0:T(128)} %get-tuple-element.99, s32[1]{0:T(128)} %get-tuple-element.98, ...), dimensions={0} | concatenate | bytes 128 | tf_op jit(solution)/shard_map/stack | solution.py:648
  141.0 0.4 collective-permute-start.16
  141.4 5.2 %collective-permute-done.16 = bf16[8,1,3,16,128]{4,3,2,1,0:T(8,128)(2,1)S(1)} collective-permute-done((bf16[8,1,3,16,128]{4,3,2,1,0:T(8,128)(2,1)S(1)}, bf16[8,1,3,16,128]{4,3,2,1,0:T(8,128)(2,1)S(1)}, u32[]{:S(2)}, u32[]{:S(2)}) %collective-permute-start.16) | collective-permute-done | bytes 98336 | tf_op jit(solution)/shard_map/ppermute | solution.py:608
  146.6 0.3 multiply_reduce_fusion
  146.9 0.7 constant_dynamic-update-slice_fusion.15
  147.6 0.4 collective-permute-start.17
  148.0 5.2 %collective-permute-done.17 = bf16[1,3,8,16,128]{4,3,2,1,0:T(8,128)(2,1)S(1)} collective-permute-done((bf16[1,3,8,16,128]{4,3,2,1,0:T(8,128)(2,1)S(1)}, bf16[1,3,8,16,128]{4,3,2,1,0:T(8,128)(2,1)S(1)}, u32[]{:S(2)}, u32[]{:S(2)}) %collective-permute-start.17) | collective-permute-done | bytes 98336 | tf_op jit(solution)/shard_map/ppermute | solution.py:608
  153.3 2.6 collective-permute-start.18
  155.9 1.0 copy-done.3
  156.9 30.8 %attend_back.1.g = bf16[3,512,1024]{2,1,0:T(8,128)(2,1)} custom-call(bf16[512,3072]{1,0:T(8,128)(2,1)} %get-tuple-element.30.q.k0.v0.q0, bf16[512,3072]{1,0:T(8,128)(2,1)} %get-tuple-element.30.q.k0.v0.q0, bf16[512,3072]{1,0:T(8,128)(2,1)} %get-tuple-element.30.q.k0.v0.q0, bf16[512,3072]{1,0:T(8,128)(2,1)} %get-tuple-element.31.k1.v1.q1, ...), custom_call_target="tpu_custom_call" | custom-call | flops 12884901888 | bytes 8388608 | tf_op jit(solution)/shard_map/attend_back/pallas_call | solution.py:486
  187.7 5.7 %qkv_grad.1 = (bf16[32,1,16,128]{3,2,1,0:T(8,128)(2,1)}, bf16[512,16]{1,0:T(8,128)(2,1)}) custom-call(s32[2]{0:T(128)} %pad_add_fusion.at, bf16[3,512,1024]{2,1,0:T(8,128)(2,1)} %attend_back.1.g, bf16[512,16]{1,0:T(8,128)(2,1)} %get-tuple-element.37.low, bf16[512,1024]{1,0:T(8,128)(2,1)} %bitcast.39, f32[1,1024]{1,0:T(1,128)} %bitcast.52, ...), custom_call_target="tpu_custom_call" | custom-call | flops 201326592 | bytes 4194304 | tf_op jit(solution)/shard_map/qkv_grad/pallas_call | solution.py:538
  193.4 1.0 fusion.13
  194.4 1.2 collective-permute-done.2
  195.7 0.6 collective-permute-start.3
  196.3 0.6 collective-permute-start.19
  197.0 3.1 %collective-permute-done.3 = bf16[2,8,1,16,128]{4,3,1,2,0:T(8,128)(2,1)S(1)} collective-permute-done((bf16[2,8,1,16,128]{4,3,1,2,0:T(8,128)(2,1)S(1)}, bf16[2,8,1,16,128]{4,3,1,2,0:T(8,128)(2,1)S(1)}, u32[]{:S(2)}, u32[]{:S(2)}) %collective-permute-start.3) | collective-permute-done | bytes 65568 | tf_op jit(solution)/shard_map/ppermute | solution.py:608
  200.1 0.7 collective-permute-start.4
  200.8 7.2 %collective-permute-done.4 = bf16[2,4,1,16,128]{4,3,1,2,0:T(8,128)(2,1)S(1)} collective-permute-done((bf16[2,4,1,16,128]{4,3,1,2,0:T(8,128)(2,1)S(1)}, bf16[2,4,1,16,128]{4,3,1,2,0:T(8,128)(2,1)S(1)}, u32[]{:S(2)}, u32[]{:S(2)}) %collective-permute-start.4) | collective-permute-done | bytes 32800 | tf_op jit(solution)/shard_map/ppermute | solution.py:608
  208.0 0.1 collective-permute-start.5
  208.1 0.1 pad_maximum_fusion
  208.2 1.6 collective-permute-start.20
  209.8 2.2 collective-permute-done.5
  212.0 0.5 collective-permute-start.6
  212.4 0.1 constant_dynamic-update-slice_fusion.13
  212.5 4.3 %collective-permute-done.6 = bf16[8,1,1,16,128]{4,3,1,2,0:T(8,128)(2,1)S(1)} collective-permute-done((bf16[8,1,1,16,128]{4,3,1,2,0:T(8,128)(2,1)S(1)}, bf16[8,1,1,16,128]{4,3,1,2,0:T(8,128)(2,1)S(1)}, u32[]{:S(2)}, u32[]{:S(2)}) %collective-permute-start.6) | collective-permute-done | bytes 32800 | tf_op jit(solution)/shard_map/ppermute | solution.py:608
  216.9 0.2 multiply_reduce_fusion.1
  217.1 0.6 collective-permute-start.7
  217.6 0.2 constant_dynamic-update-slice_fusion.12
  217.9 4.1 %collective-permute-done.7 = bf16[1,1,8,16,128]{4,3,2,1,0:T(8,128)(2,1)S(1)} collective-permute-done((bf16[1,1,8,16,128]{4,3,2,1,0:T(8,128)(2,1)S(1)}, bf16[1,1,8,16,128]{4,3,2,1,0:T(8,128)(2,1)S(1)}, u32[]{:S(2)}, u32[]{:S(2)}) %collective-permute-start.7) | collective-permute-done | bytes 32800 | tf_op jit(solution)/shard_map/ppermute | solution.py:608
  222.0 0.1 collective-permute-start.8
  222.1 4.6 %collective-permute-done.20 = bf16[8,3,8,16,128]{4,3,2,1,0:T(8,128)(2,1)S(1)} collective-permute-done((bf16[8,3,8,16,128]{4,3,2,1,0:T(8,128)(2,1)S(1)}, bf16[8,3,8,16,128]{4,3,2,1,0:T(8,128)(2,1)S(1)}, u32[]{:S(2)}, u32[]{:S(2)}) %collective-permute-start.20) | collective-permute-done | bytes 786464 | tf_op jit(solution)/shard_map/ppermute | solution.py:608
  226.6 0.5 constant_dynamic-update-slice_fusion.11
  227.2 0.6 collective-permute-start.9
  227.8 5.3 %collective-permute-done.9 = bf16[4,1,8,16,128]{4,3,2,1,0:T(8,128)(2,1)S(1)} collective-permute-done((bf16[4,1,8,16,128]{4,3,2,1,0:T(8,128)(2,1)S(1)}, bf16[4,1,8,16,128]{4,3,2,1,0:T(8,128)(2,1)S(1)}, u32[]{:S(2)}, u32[]{:S(2)}) %collective-permute-start.9) | collective-permute-done | bytes 131104 | tf_op jit(solution)/shard_map/ppermute | solution.py:608
  233.2 1.6 collective-permute-start.10
  234.9 6.3 %collective-permute-done.10 = bf16[8,1,8,16,128]{4,3,2,1,0:T(8,128)(2,1)S(1)} collective-permute-done((bf16[8,1,8,16,128]{4,3,2,1,0:T(8,128)(2,1)S(1)}, bf16[8,1,8,16,128]{4,3,2,1,0:T(8,128)(2,1)S(1)}, u32[]{:S(2)}, u32[]{:S(2)}) %collective-permute-start.10) | collective-permute-done | bytes 262176 | tf_op jit(solution)/shard_map/ppermute | solution.py:608
  241.2 0.1 constant_dynamic-update-slice_fusion
  241.4 1.9 collective-permute-done.11
  243.4 0.9 copy-done.1
  244.3 0.4 constant_dynamic-update-slice_fusion.16.pieces
  244.7 12.7 %input_grad.1 = f32[512,1024]{1,0:T(8,128)} custom-call(s32[2]{0:T(128)} %pad_add_fusion.at, bf16[3,512,1024]{2,1,0:T(8,128)(2,1)} %attend_back.1.g, bf16[1024,3072]{1,0:T(8,128)(2,1)} %w.5, bf16[512,16]{1,0:T(8,128)(2,1)} %get-tuple-element.38.rank_grad, bf16[8,16,1024]{2,1,0:T(8,128)(2,1)} %down.5, bf16[512,1024]{1,0:T(8,128)(2,1)} %bitcast.40, ...), custom_call_target="tpu_custom_call" | custom-call | flops 3221225472 | bytes 14680064 | tf_op jit(solution)/shard_map/input_grad/pallas_call | solution.py:582
  257.4 3.4 %spread.2 = (f32[8,16,3072]{2,1,0:T(8,128)}, f32[8,16,1024]{2,1,0:T(8,128)}) custom-call(s32[2]{0:T(128)} %pad_add_fusion.at, bf16[32,1,8,16,128]{4,3,2,1,0:T(8,128)(2,1)} %copy-done.1), custom_call_target="tpu_custom_call" | custom-call | flops 1 | bytes 3145728 | tf_op jit(solution)/shard_map/spread/pallas_call | solution.py:671
  260.8 5.5 %spread.3 = (f32[8,16,4096]{2,1,0:T(8,128)}, f32[8,16,4096]{2,1,0:T(8,128)}, f32[8,16,1024]{2,1,0:T(8,128)}, f32[8,16,1024]{2,1,0:T(8,128)}, f32[8,16,1024]{2,1,0:T(8,128)}, /*index=5*/f32[8,16,1024]{2,1,0:T(8,128)}) custom-call(s32[2]{0:T(128)} %pad_add_fusion.at, bf16[32,3,8,16,128]{4,3,2,1,0:T(8,128)(2,1)} %copy-done), custom_call_target="tpu_custom_call" | custom-call | flops 1 | bytes 9437184 | tf_op jit(solution)/shard_map/spread/pallas_call | solution.py:671
  (45 shorter events, 0.9 us)
Async XLA Ops:
  0.6 26.4 %collective-permute-start = (bf16[512,1024]{1,0:T(8,128)(2,1)}, bf16[512,1024]{1,0:T(8,128)(2,1)S(1)}, u32[]{:S(2)}, u32[]{:S(2)}) collective-permute-start(bf16[512,1024]{1,0:T(8,128)(2,1)} %bitcast.36), channel_id=1, source_target_pairs={{1,0},{0,1},{3,2},{2,3},{5,4},{4,5},{7,6},{6,7},{9,8},{8,9},{11,10... | collective-permute-start | bytes 3145736 | tf_op jit(solution)/shard_map/ppermute | solution.py:702
  27.0 1.0 copy-start.4
  54.8 62.6 %copy-start.5 = (u32[32]{0:T(128)S(1)}, u32[32]{0:T(128)}, u32[]{:S(2)}) copy-start(u32[32]{0:T(128)} %constant.68) | copy-start | bytes 388
  100.7 1.5 collective-permute-start.12
  102.2 7.0 %collective-permute-start.13 = (bf16[2,8,3,16,128]{4,3,2,1,0:T(8,128)(2,1)S(1)}, bf16[2,8,3,16,128]{4,3,2,1,0:T(8,128)(2,1)S(1)}, u32[]{:S(2)}, u32[]{:S(2)}) collective-permute-start(bf16[2,8,3,16,128]{4,3,2,1,0:T(8,128)(2,1)S(1)} %pad_maximum_fusion.3), channel_id=1, source_target_pairs={{0,1},{1,0},{2,3},{3,2},{4,5},{5,4},{6,7},{7,6},{8,9},{9,8},{10,11... | collective-permute-start | bytes 589832 | tf_op jit(solution)/shard_map/ppermute | solution.py:608
  109.3 4.7 %collective-permute-start.14 = (bf16[2,4,3,16,128]{4,3,2,1,0:T(8,128)(2,1)S(1)}, bf16[2,4,3,16,128]{4,3,2,1,0:T(8,128)(2,1)S(1)}, u32[]{:S(2)}, u32[]{:S(2)}) collective-permute-start(bf16[2,4,3,16,128]{4,3,2,1,0:T(8,128)(2,1)S(1)} %get-tuple-element.71), channel_id=1, source_target_pairs={{0,4},{2,6},{4,0},{6,2},{8,12},{10,14},{12,8},{14,10},{16,20},{18,... | collective-permute-start | bytes 294920 | tf_op jit(solution)/shard_map/ppermute | solution.py:608
  114.0 26.9 %collective-permute-start.15 = (bf16[4,2,3,16,128]{4,3,2,1,0:T(8,128)(2,1)S(1)}, bf16[4,2,3,16,128]{4,3,2,1,0:T(8,128)(2,1)S(1)}, u32[]{:S(2)}, u32[]{:S(2)}) collective-permute-start(bf16[4,2,3,16,128]{4,3,2,1,0:T(8,128)(2,1)S(1)} %get-tuple-element.69), channel_id=1, source_target_pairs={{0,8},{2,10},{4,12},{6,14},{8,0},{10,2},{12,4},{14,6},{16,24},{18,... | collective-permute-start | bytes 294920 | tf_op jit(solution)/shard_map/ppermute | solution.py:608
  115.9 39.9 %collective-permute-start.1 = (bf16[560,1024]{1,0:T(8,128)(2,1)}, bf16[560,1024]{1,0:T(8,128)(2,1)S(1)}, u32[]{:S(2)}, u32[]{:S(2)}) collective-permute-start(bf16[560,1024]{1,0:T(8,128)(2,1)} %get-tuple-element.35.go), channel_id=1, source_target_pairs={{1,0},{0,1},{3,2},{2,3},{5,4},{4,5},{7,6},{6,7},{9,8},{8,9},{11,10... | collective-permute-start | bytes 3440648 | tf_op jit(solution)/shard_map/ppermute | solution.py:702
  141.0 5.6 %collective-permute-start.16 = (bf16[8,1,3,16,128]{4,3,2,1,0:T(8,128)(2,1)S(1)}, bf16[8,1,3,16,128]{4,3,2,1,0:T(8,128)(2,1)S(1)}, u32[]{:S(2)}, u32[]{:S(2)}) collective-permute-start(bf16[8,1,3,16,128]{4,3,2,1,0:T(8,128)(2,1)S(1)} %get-tuple-element.67), channel_id=1, source_target_pairs={{0,16},{2,18},{4,20},{6,22},{8,24},{10,26},{12,28},{14,30},{16,0},... | collective-permute-start | bytes 294920 | tf_op jit(solution)/shard_map/ppermute | solution.py:608
  147.6 5.6 %collective-permute-start.17 = (bf16[1,3,8,16,128]{4,3,2,1,0:T(8,128)(2,1)S(1)}, bf16[1,3,8,16,128]{4,3,2,1,0:T(8,128)(2,1)S(1)}, u32[]{:S(2)}, u32[]{:S(2)}) collective-permute-start(bf16[1,3,8,16,128]{4,3,2,1,0:T(8,128)(2,1)S(1)} %get-tuple-element.51), channel_id=1, source_target_pairs={{0,16},{2,18},{4,20},{6,22},{8,24},{10,26},{12,28},{14,30},{16,0},... | collective-permute-start | bytes 294920 | tf_op jit(solution)/shard_map/ppermute | solution.py:608
  153.3 43.0 %collective-permute-start.18 = (bf16[2,3,8,16,128]{4,3,2,1,0:T(8,128)(2,1)S(1)}, bf16[2,3,8,16,128]{4,3,2,1,0:T(8,128)(2,1)S(1)}, u32[]{:S(2)}, u32[]{:S(2)}) collective-permute-start(bf16[2,3,8,16,128]{4,3,2,1,0:T(8,128)(2,1)S(1)} %pad_maximum_fusion.4), channel_id=1, source_target_pairs={{0,8},{2,10},{4,12},{6,14},{8,0},{10,2},{12,4},{14,6},{16,24},{18,... | collective-permute-start | bytes 589832 | tf_op jit(solution)/shard_map/ppermute | solution.py:608
  155.9 1.0 copy-start.3
  193.4 16.4 %copy-start.2 = (bf16[16,3,8,16,128]{4,3,2,1,0:T(8,128)(2,1)S(1)}, bf16[16,3,8,16,128]{4,3,2,1,0:T(8,128)(2,1)}, u32[]{:S(2)}) copy-start(bf16[16,3,8,16,128]{4,3,2,1,0:T(8,128)(2,1)} %get-tuple-element.50) | copy-start | bytes 4718596
  194.4 1.3 collective-permute-start.2
  195.7 4.3 %collective-permute-start.3 = (bf16[2,8,1,16,128]{4,3,1,2,0:T(8,128)(2,1)S(1)}, bf16[2,8,1,16,128]{4,3,1,2,0:T(8,128)(2,1)S(1)}, u32[]{:S(2)}, u32[]{:S(2)}) collective-permute-start(bf16[2,8,1,16,128]{4,3,1,2,0:T(8,128)(2,1)S(1)} %pad_maximum_fusion.8), channel_id=1, source_target_pairs={{0,1},{1,0},{2,3},{3,2},{4,5},{5,4},{6,7},{7,6},{8,9},{9,8},{10,11... | collective-permute-start | bytes 196616 | tf_op jit(solution)/shard_map/ppermute | solution.py:608
  196.3 11.7 %collective-permute-start.19 = (bf16[4,3,8,16,128]{4,3,2,1,0:T(8,128)(2,1)S(1)}, bf16[4,3,8,16,128]{4,3,2,1,0:T(8,128)(2,1)S(1)}, u32[]{:S(2)}, u32[]{:S(2)}) collective-permute-start(bf16[4,3,8,16,128]{4,3,2,1,0:T(8,128)(2,1)S(1)} %pad_maximum_fusion.1), channel_id=1, source_target_pairs={{0,4},{2,6},{4,0},{6,2},{8,12},{10,14},{12,8},{14,10},{16,20},{18,... | collective-permute-start | bytes 1179656 | tf_op jit(solution)/shard_map/ppermute | solution.py:608
  200.1 7.9 %collective-permute-start.4 = (bf16[2,4,1,16,128]{4,3,1,2,0:T(8,128)(2,1)S(1)}, bf16[2,4,1,16,128]{4,3,1,2,0:T(8,128)(2,1)S(1)}, u32[]{:S(2)}, u32[]{:S(2)}) collective-permute-start(bf16[2,4,1,16,128]{4,3,1,2,0:T(8,128)(2,1)S(1)} %get-tuple-element.85), channel_id=1, source_target_pairs={{0,4},{2,6},{4,0},{6,2},{8,12},{10,14},{12,8},{14,10},{16,20},{18,... | collective-permute-start | bytes 98312 | tf_op jit(solution)/shard_map/ppermute | solution.py:608
  208.0 4.0 %collective-permute-start.5 = (bf16[4,2,1,16,128]{4,3,1,2,0:T(8,128)(2,1)S(1)}, bf16[4,2,1,16,128]{4,3,1,2,0:T(8,128)(2,1)S(1)}, u32[]{:S(2)}, u32[]{:S(2)}) collective-permute-start(bf16[4,2,1,16,128]{4,3,1,2,0:T(8,128)(2,1)S(1)} %get-tuple-element.83), channel_id=1, source_target_pairs={{0,8},{2,10},{4,12},{6,14},{8,0},{10,2},{12,4},{14,6},{16,24},{18,... | collective-permute-start | bytes 98312 | tf_op jit(solution)/shard_map/ppermute | solution.py:608
  208.2 18.5 %collective-permute-start.20 = (bf16[8,3,8,16,128]{4,3,2,1,0:T(8,128)(2,1)S(1)}, bf16[8,3,8,16,128]{4,3,2,1,0:T(8,128)(2,1)S(1)}, u32[]{:S(2)}, u32[]{:S(2)}) collective-permute-start(bf16[8,3,8,16,128]{4,3,2,1,0:T(8,128)(2,1)S(1)} %pad_maximum_fusion), channel_id=1, source_target_pairs={{0,1},{1,0},{2,3},{3,2},{4,5},{5,4},{6,7},{7,6},{8,9},{9,8},{10,11... | collective-permute-start | bytes 2359304 | tf_op jit(solution)/shard_map/ppermute | solution.py:608
  212.0 4.9 %collective-permute-start.6 = (bf16[8,1,1,16,128]{4,3,1,2,0:T(8,128)(2,1)S(1)}, bf16[8,1,1,16,128]{4,3,1,2,0:T(8,128)(2,1)S(1)}, u32[]{:S(2)}, u32[]{:S(2)}) collective-permute-start(bf16[8,1,1,16,128]{4,3,1,2,0:T(8,128)(2,1)S(1)} %get-tuple-element.81), channel_id=1, source_target_pairs={{0,16},{2,18},{4,20},{6,22},{8,24},{10,26},{12,28},{14,30},{16,0},... | collective-permute-start | bytes 98312 | tf_op jit(solution)/shard_map/ppermute | solution.py:608
  217.1 4.9 %collective-permute-start.7 = (bf16[1,1,8,16,128]{4,3,2,1,0:T(8,128)(2,1)S(1)}, bf16[1,1,8,16,128]{4,3,2,1,0:T(8,128)(2,1)S(1)}, u32[]{:S(2)}, u32[]{:S(2)}) collective-permute-start(bf16[1,1,8,16,128]{4,3,2,1,0:T(8,128)(2,1)S(1)} %bitcast.42), channel_id=1, source_target_pairs={{0,16},{2,18},{4,20},{6,22},{8,24},{10,26},{12,28},{14,30},{16,0},... | collective-permute-start | bytes 98312 | tf_op jit(solution)/shard_map/ppermute | solution.py:608
  222.0 5.2 %collective-permute-start.8 = (bf16[2,1,8,16,128]{4,3,2,1,0:T(8,128)(2,1)S(1)}, bf16[2,1,8,16,128]{4,3,2,1,0:T(8,128)(2,1)S(1)}, u32[]{:S(2)}, u32[]{:S(2)}) collective-permute-start(bf16[2,1,8,16,128]{4,3,2,1,0:T(8,128)(2,1)S(1)} %pad_maximum_fusion.9), channel_id=1, source_target_pairs={{0,8},{2,10},{4,12},{6,14},{8,0},{10,2},{12,4},{14,6},{16,24},{18,... | collective-permute-start | bytes 196616 | tf_op jit(solution)/shard_map/ppermute | solution.py:608
  227.1 16.3 %collective-permute-start.21 = (bf16[16,3,8,16,128]{4,3,2,1,0:T(8,128)(2,1)S(1)}, bf16[16,3,8,16,128]{4,3,2,1,0:T(8,128)(2,1)S(1)}, u32[]{:S(2)}, u32[]{:S(2)}) collective-permute-start(bf16[16,3,8,16,128]{4,3,2,1,0:T(8,128)(2,1)S(1)} %get-tuple-element.52), channel_id=1, source_target_pairs={{0,2},{2,0},{4,6},{6,4},{8,10},{10,8},{12,14},{14,12},{16,18},{18,... | collective-permute-start | bytes 4718600 | tf_op jit(solution)/shard_map/ppermute | solution.py:608
  227.2 6.0 %collective-permute-start.9 = (bf16[4,1,8,16,128]{4,3,2,1,0:T(8,128)(2,1)S(1)}, bf16[4,1,8,16,128]{4,3,2,1,0:T(8,128)(2,1)S(1)}, u32[]{:S(2)}, u32[]{:S(2)}) collective-permute-start(bf16[4,1,8,16,128]{4,3,2,1,0:T(8,128)(2,1)S(1)} %pad_maximum_fusion.5), channel_id=1, source_target_pairs={{0,4},{2,6},{4,0},{6,2},{8,12},{10,14},{12,8},{14,10},{16,20},{18,... | collective-permute-start | bytes 393224 | tf_op jit(solution)/shard_map/ppermute | solution.py:608
  233.2 8.0 %collective-permute-start.10 = (bf16[8,1,8,16,128]{4,3,2,1,0:T(8,128)(2,1)S(1)}, bf16[8,1,8,16,128]{4,3,2,1,0:T(8,128)(2,1)S(1)}, u32[]{:S(2)}, u32[]{:S(2)}) collective-permute-start(bf16[8,1,8,16,128]{4,3,2,1,0:T(8,128)(2,1)S(1)} %pad_maximum_fusion.2), channel_id=1, source_target_pairs={{0,1},{1,0},{2,3},{3,2},{4,5},{5,4},{6,7},{7,6},{8,9},{9,8},{10,11... | collective-permute-start | bytes 786440 | tf_op jit(solution)/shard_map/ppermute | solution.py:608
  241.3 2.0 collective-permute-start.11
  243.4 1.0 copy-start.1
  244.7 12.7 %copy-start = (bf16[32,3,8,16,128]{4,3,2,1,0:T(8,128)(2,1)}, bf16[32,3,8,16,128]{4,3,2,1,0:T(8,128)(2,1)S(1)}, u32[]{:S(2)}) copy-start(bf16[32,3,8,16,128]{4,3,2,1,0:T(8,128)(2,1)S(1)} %constant_dynamic-update-slice_fusion.16.pieces) | copy-start | bytes 9437188
